TPU v7x, 32 devices: a whole 2x2x4 slice. The times are simulated.
32 devices in a mesh: groups: 2 (over y), rows: 4 (over z), cols: 2 (over x), sub: 2 (over core).
Axes of the slice: x: 2, y: 2, z: 4, core: 2. Of those that a mesh axis runs over, the one named last changes fastest.
Arguments:
- latents: bfloat16 [16, 8, 768], P(('groups', 'rows', 'cols'), None, 'sub'), parts along dimension 0, may hold values from -36 to 36
- timestep: int32 [2], P('groups'), parts along dimension 0, may hold values from 0 to 999
- scan_order: int32 [8], replicated, may hold values from 0 to 7, each once
- modulation: bfloat16 [128, 3, 768], P(None, None, 'sub'), may hold values from -0.5 to 0.5
- input_proj: bfloat16 [768, 2, 1536], P(None, None, 'sub'), may hold values from -0.21875 to 0.21875
- conv_weight: float32 [4, 1536], P(None, 'sub'), may hold values from -3 to 3
- conv_bias: float32 [1536], P('sub'), may hold values from -2 to 2
- select_proj: bfloat16 [1536, 80], P('sub'), may hold values from -0.15625 to 0.15625
- step_proj: bfloat16 [48, 1536], P(None, 'sub'), may hold values from -0.875 to 0.875
- step_bias: float32 [1536], P('sub'), may hold values from -6 to -1
- decay_log: float32 [16, 1536], P(None, 'sub'), may hold values from 0 to 2.77
- skip_gain: float32 [1536], P('sub'), may hold values from 0.5 to 2
- output_proj: bfloat16 [1536, 768], P('sub'), may hold values from -0.15625 to 0.15625
Outputs:
- blended: bfloat16 [16, 8, 768], P(('groups', 'rows', 'cols'), None, 'sub'), parts along dimension 0
There are 2 independent parts, one for each index of `groups`. A program takes and returns all parts, laid end to end along the dimension named above; an argument that names none is the same for every part. Nothing has to cross between parts.
All inputs are finite; a program needn't handle non-finite values.
Results may differ from a plain program's by a relative error of at most 0.0065.
Values may be sent and summed in bfloat16 or wider, within the bound.
No kernel may reach another device: no remote copies, remote signals or barrier semaphores. Data moves between devices by JAX's collectives and lax.ppermute only.
A program may use at most 64 MiB of HBM per device.

v0:
```python
import math

import jax
import jax.numpy as jnp
from jax import lax
from jax.sharding import PartitionSpec as P

NS = 16
RANK = 48


EPSILON = 1e-06


def embed_time(timestep, freq_count):
    halfway = freq_count // 2
    frequency = jnp.exp(-math.log(10000.0) * jnp.arange(halfway, dtype=jnp.float32) / halfway)
    angles = timestep.astype(jnp.float32)[0] * frequency
    return jnp.concatenate([jnp.cos(angles), jnp.sin(angles)]).astype(jnp.bfloat16)


def widen(latent_half, scale_shift):
    return (
        lax.all_gather(latent_half, "sub", axis=2, tiled=True),
        lax.all_gather(scale_shift, "sub", axis=1, tiled=True),
    )


def normalize(latent_full, scale_full):
    values = latent_full.astype(jnp.float32)
    meansq = jnp.mean(values * values, axis=-1, keepdims=True)
    scaled = values * lax.rsqrt(meansq + EPSILON)
    scale_row = scale_full[0].astype(jnp.float32)
    shift_row = scale_full[1].astype(jnp.float32)
    return (scaled * (1.0 + scale_row) + shift_row).astype(jnp.bfloat16)


def project_in(normed, input_proj):
    model_width = input_proj.shape[0]
    flat_weight = input_proj.reshape(model_width, -1)
    result = jnp.dot(
        normed.reshape(-1, model_width), flat_weight, preferred_element_type=jnp.float32
    )
    return result.astype(jnp.bfloat16).reshape(normed.shape[:-1] + (flat_weight.shape[1],))


def reorder(one_hot, sequence):
    return jnp.einsum("kh,hnc->knc", one_hot, sequence, preferred_element_type=jnp.float32).astype(
        jnp.bfloat16
    )


def restore(one_hot, sequence):
    return jnp.einsum("kh,knc->hnc", one_hot, sequence, preferred_element_type=jnp.float32).astype(
        jnp.bfloat16
    )


def scan_columns(
    projected, conv_weight, conv_bias, select_proj, step_proj, step_bias, decay_log, skip_gain
):
    height, item_count, doubled = projected.shape
    inner_width = doubled // 2
    seq_input = projected[..., :inner_width].astype(jnp.float32)
    seq_gate = projected[..., inner_width:].astype(jnp.float32)
    tap_count = conv_weight.shape[0]
    padded = jnp.pad(seq_input, ((tap_count - 1, 0), (0, 0), (0, 0)))
    conv_sum = conv_bias + jnp.zeros_like(seq_input)
    for offset in range(tap_count):
        conv_sum = conv_sum + conv_weight[offset] * padded[offset : offset + height]
    activated = jax.nn.silu(conv_sum).astype(jnp.bfloat16)
    flat_act = activated.reshape(height * item_count, inner_width)
    partial_value = lax.dot_general(
        select_proj, flat_act, (((0,), (1,)), ((), ())), preferred_element_type=jnp.float32
    )
    selected = lax.psum(partial_value, "sub")
    step_low = selected[:RANK].astype(jnp.bfloat16)
    step_pre = lax.dot_general(
        step_low, step_proj, (((0,), (0,)), ((), ())), preferred_element_type=jnp.float32
    )
    step_size = jax.nn.softplus(step_pre + step_bias).reshape(height, item_count, inner_width)
    entry_coef = selected[RANK : RANK + NS].T.reshape(height, item_count, NS)
    exit_coef = selected[RANK + NS :].T.reshape(height, item_count, NS)
    act_float = activated.astype(jnp.float32)
    decay_rate = -jnp.exp(decay_log)
    block_len = height // 16 if height % 16 == 0 else height
    blocks = height // block_len

    def split_blocks(tensor):
        return tensor.reshape((blocks, block_len) + tensor.shape[1:])

    def combine(earlier, latter):
        return (earlier[0] * latter[0], latter[0] * earlier[1] + latter[1])

    def advance(carried, pieces):
        step_blk, act_blk, entry_blk, exit_blk = pieces
        decays = jnp.exp(step_blk[:, :, None, :] * decay_rate)
        driving = (step_blk * act_blk)[:, :, None, :] * entry_blk[..., None]
        cum_decay, cum_drive = lax.associative_scan(combine, (decays, driving), axis=0)
        states = cum_drive + cum_decay * carried[None]
        output = jnp.sum(exit_blk[..., None] * states, axis=2) + skip_gain * act_blk
        return (states[-1], output)

    initial = jnp.zeros((item_count, NS, inner_width), jnp.float32)
    pieces_all = (
        split_blocks(step_size),
        split_blocks(act_float),
        split_blocks(entry_coef),
        split_blocks(exit_coef),
    )
    _, outputs = lax.scan(advance, initial, pieces_all)
    scanned = outputs.reshape(height, item_count, inner_width)
    return (scanned * jax.nn.silu(seq_gate)).astype(jnp.bfloat16)


def on_device(
    latents,
    timestep,
    scan_order,
    modulation,
    input_proj,
    conv_weight,
    conv_bias,
    select_proj,
    step_proj,
    step_bias,
    decay_log,
    skip_gain,
    output_proj,
):
    rows_dev, grid_width, half_model = latents.shape
    line_groups = lax.axis_size(("rows", "cols"))
    cols_dev = grid_width // line_groups
    height = rows_dev * line_groups
    inner_width = input_proj.shape[2]
    freq_count = modulation.shape[0]
    time_embed = embed_time(timestep, freq_count)
    mod_rows = jnp.dot(
        time_embed[None, :], modulation.reshape(freq_count, -1), preferred_element_type=jnp.float32
    )
    mod_rows = mod_rows.reshape(3, half_model).astype(jnp.bfloat16)
    scale_shift = mod_rows[:2]
    gate_row = mod_rows[2].astype(jnp.float32)
    one_hot = (scan_order[:, None] == jnp.arange(height, dtype=jnp.int32)[None, :]).astype(
        jnp.bfloat16
    )
    latent_full, scale_full = widen(latents, scale_shift)
    projected = project_in(normalize(latent_full, scale_full), input_proj)
    sectioned = projected.reshape(rows_dev, line_groups, cols_dev, 2 * inner_width)[None]
    received = lax.all_to_all(sectioned, ("rows", "cols"), split_axis=2, concat_axis=0, tiled=True)
    item_count = received.shape[3]
    ordered = reorder(one_hot, received.reshape(height, item_count, 2 * inner_width))
    gated = scan_columns(
        ordered, conv_weight, conv_bias, select_proj, step_proj, step_bias, decay_log, skip_gain
    )
    placed = restore(one_hot, gated)
    returned = lax.all_to_all(
        placed.reshape(line_groups, rows_dev, 1, item_count, inner_width),
        ("rows", "cols"),
        split_axis=0,
        concat_axis=2,
        tiled=True,
    )
    gathered = returned.reshape(rows_dev, line_groups, item_count, inner_width)
    partial_value = jnp.dot(
        gathered.reshape(rows_dev * grid_width, inner_width),
        output_proj,
        preferred_element_type=jnp.float32,
    )
    summed = lax.psum_scatter(
        partial_value.reshape(rows_dev, grid_width, -1).astype(jnp.bfloat16),
        "sub",
        scatter_dimension=2,
        tiled=True,
    )
    blended = latents.astype(jnp.float32) + gate_row * summed.astype(jnp.float32)
    return blended.astype(jnp.bfloat16)


def solution(mesh):
    placed = (
        P(("groups", "rows", "cols"), None, "sub"),
        P("groups"),
        P(),
        P(None, None, "sub"),
        P(None, None, "sub"),
        P(None, "sub"),
        P("sub"),
        P("sub", None),
        P(None, "sub"),
        P("sub"),
        P(None, "sub"),
        P("sub"),
        P("sub", None),
    )
    return jax.shard_map(
        on_device,
        mesh=mesh,
        in_specs=placed,
        out_specs=P(("groups", "rows", "cols"), None, "sub"),
        check_vma=False,
    )
```

profile of v0, /device:TPU:0, one launch (start us, length us, event | category | flops | bytes accessed | tf_op | source)
XLA Modules:
  0.0 60.8 jit_solution(16763260327441365407)
XLA Ops:
  7.3 1.2 %copy.21 = bf16[128,3,384]{0,2,1:T(8,128)(2,1)S(1)} copy(bf16[128,3,384]{2,0,1:T(8,128)(2,1)} %param.16) | data formatting | bytes 589824 | tf_op args[3]
  8.5 0.2 fusion.4
  8.8 2.0 %all_gather.7 = bf16[2,768]{1,0:T(2,128)(2,1)S(1)} all-gather(bf16[2,384]{1,0:T(2,128)(2,1)S(1)} %slice.199), channel_id=1, replica_groups=mesh['groups'=2,'rows'=4,'cols'=2,'sub'=2] {'sub'}, dimensions={1}, use_global_device_ids=true | all-gather | bytes 4608 | tf_op jit(solution)/shard_map/all_gather | solution.py:25
  10.8 2.0 %all_gather.6 = bf16[1,8,768]{2,1,0:T(8,128)(2,1)S(1)} all-gather(bf16[1,8,384]{2,1,0:T(8,128)(2,1)} %param.13), channel_id=1, replica_groups=mesh['groups'=2,'rows'=4,'cols'=2,'sub'=2] {'sub'}, dimensions={2}, use_global_device_ids=true | all-gather | bytes 18432 | tf_op jit(solution)/shard_map/all_gather | solution.py:24
  12.8 0.1 fusion.12
  13.0 2.1 %copy.30 = bf16[96,8,2,768]{3,1,2,0:T(8,128)(2,1)S(1)} copy(bf16[96,8,2,768]{3,2,1,0:T(2,128)(2,1)} %bitcast.69) | data formatting | bytes 4718592
  15.1 0.4 fusion
  15.6 0.5 broadcast.127
  16.2 0.8 %reduce.16 = bf16[8,1536]{1,0:T(8,128)(2,1)S(1)} reduce(bf16[8,1,1,1,1536]{4,3,2,1,0:T(2,128)(2,1)S(1)} %bitcast.72, bf16[]{:T(256)} %broadcast.127), dimensions={1,2,3}, to_apply=%bitcast.67.reduce_sub_computation | reduce | bytes 49154
  16.9 0.6 %reshape.175 = bf16[8,2,768]{2,1,0:T(2,128)(2,1)} reshape(bf16[8,1536]{1,0:T(8,128)(2,1)S(1)} %reduce.16) | data formatting | bytes 49152
  17.6 7.1 %all-to-all-start = ((bf16[8,2,768]{2,1,0:T(2,128)(2,1)}), bf16[8,2,768]{2,1,0:T(2,128)(2,1)S(1)}, u32[]{:S(2)}, u32[]{:S(2)}) async-start(bf16[8,2,768]{2,1,0:T(2,128)(2,1)} %reshape.175), calls=%async_computation | async-start | bytes 49152 | tf_op jit(solution)/shard_map/all_to_all | solution.py:150
  24.8 6.5 %all-to-all-done = bf16[8,2,768]{2,1,0:T(2,128)(2,1)S(1)} async-done(((bf16[8,2,768]{2,1,0:T(2,128)(2,1)}), bf16[8,2,768]{2,1,0:T(2,128)(2,1)S(1)}, u32[]{:S(2)}, u32[]{:S(2)}) %all-to-all-start) | async-done | bytes 24608 | tf_op jit(solution)/shard_map/all_to_all | solution.py:150
  31.4 0.2 fusion.1
  31.6 0.1 convolution_bitcast_fusion
  31.7 2.5 %psum.7 = f32[80,8]{0,1:T(8,128)S(1)} all-reduce(f32[80,8]{0,1:T(8,128)S(1)} %convolution_bitcast_fusion), channel_id=1, replica_groups=mesh['groups'=2,'rows'=4,'cols'=2,'sub'=2] {'sub'}, use_global_device_ids=true, to_apply=%region_1.2 | all-reduce | flops 640 | bytes 5120 | tf_op jit(solution)/shard_map/psum | solution.py:76
  34.2 0.1 slice_bitcast_fusion.1
  34.3 0.1 compare_select_fusion
  34.5 0.1 multiply_exponential_fusion
  34.6 0.1 broadcast_multiply_fusion
  35.2 0.1 pad.60
  35.5 0.2 multiply_reduce_fusion
  35.6 0.2 copy-done.8
  35.9 0.2 fusion.2
  36.1 0.7 %reduce.17 = bf16[8,768]{1,0:T(8,128)(2,1)S(1)} reduce(bf16[8,1,1,1,768]{4,0,3,2,1:T(8,128)(2,1)S(1)} %fusion.2, bf16[]{:T(256)} %broadcast.127), dimensions={1,2,3}, to_apply=%copy.23.reduce_sub_computation | reduce | bytes 24578 | tf_op jit(solution)/shard_map/reshape | solution.py:158
  36.8 8.9 %all_to_all.8 = bf16[8,2,384]{2,1,0:T(2,128)(2,1)S(1)} all-to-all(bf16[8,2,384]{2,1,0:T(2,128)(2,1)S(1)} %reshape.177), channel_id=1, replica_groups=mesh['groups'=2,'rows'=4,'cols'=2,'sub'=2] {'rows','cols'}, dimensions={0} | all-to-all | bytes 24576 | tf_op jit(solution)/shard_map/all_to_all | solution.py:157
  45.7 0.3 fusion.3
  46.0 0.4 copy.25
  46.4 0.7 %copy.42 = bf16[768,1,8]{2,0,1:T(8,128)(2,1)} copy(bf16[768,1,8]{2,1,0:T(2,128)(2,1)S(1)} %bitcast.70) | data formatting | bytes 24576
  47.1 5.1 %reduce-scatter.4.cloned.1.call-done = bf16[384,8]{1,0:T(8,128)(2,1)} async-done(((bf16[768,8]{1,0:T(8,128)(2,1)}), bf16[384,8]{1,0:T(8,128)(2,1)}) %reduce-scatter.4.cloned.1.call-update) | async-done | bytes 6160
  52.2 1.0 %reshape_bitcast_fusion = bf16[1,8,384]{1,0,2:T(2,128)(2,1)S(1)} fusion(bf16[384,8]{1,0:T(8,128)(2,1)} %reduce-scatter.4.cloned.1.call-done), kind=kLoop, calls=%fused_computation.17 | loop fusion | bytes 12288
  53.2 0.1 copy.26
  53.3 0.6 %add_convert_fusion = bf16[1,8,384]{2,1,0:T(8,128)(2,1)} fusion(bf16[1,8,384]{2,1,0:T(8,128)(2,1)S(1)} %copy.26, bf16[1,8,384]{2,1,0:T(8,128)(2,1)S(1)} %copy-done.4, f32[384]{0:T(512)S(1)} %fusion.48), kind=kLoop, calls=%fused_computation.79 | loop fusion | flops 15360 | bytes 19968 | tf_op jit(solution)/shard_map/convert_element_type | solution.py:177
  (59 shorter events, 1.1 us)
Async XLA Ops:
  6.5 39.2 %copy-start = (bf16[768,768]{1,0:T(8,128)(2,1)S(1)}, bf16[768,768]{1,0:T(8,128)(2,1)}, u32[]{:S(2)}) copy-start(bf16[768,768]{1,0:T(8,128)(2,1)} %param.25) | copy-start | bytes 3538948
  15.1 9.7 %copy-start.3 = (f32[16,768]{1,0:T(8,128)S(1)}, f32[16,768]{1,0:T(8,128)}, u32[]{:S(2)}) copy-start(f32[16,768]{1,0:T(8,128)} %param.23) | copy-start | bytes 147460
  15.1 9.7 %copy-start.6 = (f32[4,768]{1,0:T(4,128)S(1)}, f32[4,768]{1,0:T(4,128)}, u32[]{:S(2)}) copy-start(f32[4,768]{1,0:T(4,128)} %param.18) | copy-start | bytes 36868
  15.1 16.3 %copy-start.9 = (s32[8]{0:T(128)S(1)}, s32[8]{0:T(128)}, u32[]{:S(2)}) copy-start(s32[8]{0:T(128)} %param.15) | copy-start | bytes 100
  15.1 16.5 %copy-start.5 = (f32[768]{0:T(1024)S(1)}, f32[768]{0:T(1024)}, u32[]{:S(2)}) copy-start(f32[768]{0:T(1024)} %param.19) | copy-start | bytes 9220
  15.1 16.5 %copy-start.1 = (bf16[768,80]{0,1:T(8,128)(2,1)S(1)}, bf16[768,80]{0,1:T(8,128)(2,1)}, u32[]{:S(2)}) copy-start(bf16[768,80]{0,1:T(8,128)(2,1)} %param.20) | copy-start | bytes 368644
  15.1 19.2 %copy-start.2 = (bf16[48,768]{1,0:T(8,128)(2,1)S(1)}, bf16[48,768]{1,0:T(8,128)(2,1)}, u32[]{:S(2)}) copy-start(bf16[48,768]{1,0:T(8,128)(2,1)} %param.21) | copy-start | bytes 221188
  15.1 19.2 %copy-start.7 = (f32[768]{0:T(1024)S(1)}, f32[768]{0:T(1024)}, u32[]{:S(2)}) copy-start(f32[768]{0:T(1024)} %param.22) | copy-start | bytes 9220
  17.6 13.8 %all-to-all-start = ((bf16[8,2,768]{2,1,0:T(2,128)(2,1)}), bf16[8,2,768]{2,1,0:T(2,128)(2,1)S(1)}, u32[]{:S(2)}, u32[]{:S(2)}) async-start(bf16[8,2,768]{2,1,0:T(2,128)(2,1)} %reshape.175), calls=%async_computation | async-start | bytes 49152 | tf_op jit(solution)/shard_map/all_to_all | solution.py:150
  24.7 27.6 %reduce-scatter.4.cloned.1.call-start = ((), (), s32[]{:S(2)}) async-start(), calls=%async_computation.3 | async-start | bytes 294912
  35.2 0.7 %copy-start.8 = (f32[768]{0:T(1024)S(1)}, f32[768]{0:T(1024)}, u32[]{:S(2)}) copy-start(f32[768]{0:T(1024)} %param.24) | copy-start | bytes 9220
  35.5 17.9 %copy-start.4 = (bf16[1,8,384]{2,1,0:T(8,128)(2,1)S(1)}, bf16[1,8,384]{2,1,0:T(8,128)(2,1)}, u32[]{:S(2)}) copy-start(bf16[1,8,384]{2,1,0:T(8,128)(2,1)} %param.13) | copy-start | bytes 18436
Sparse Core Ops, SparseCore 0:
  47.2 4.9 reduce-scatter.3
where the time goes:
time: 61.2 us; the launch traced here: 60.8 us
  blocking collectives  15.4 us (25%)
  between operations  14.6 us (24%)
  waiting for transfers between devices  11.6 us (19%)
  local copies, waits for them, and re-layouts  7.41 us (12%)
  starting transfers between devices  7.17 us (12%)
  other arithmetic  2.95 us (5%)
  matrix products  1.65 us (3%)
    all_to_all x1, blocking collectives, on_device(): lax.all_to_all(placed.reshape(line_groups, rows_dev, 1, item_count, inner...  8.92 us
    all_to_all x1, starting transfers between devices, on_device(): lax.all_to_all(sectioned, ('rows', 'cols'), split_axis=2, concat_axis=0,...  7.13 us
    unnamed x31, local copies, waits for them, and re-layouts  6.87 us
    all_to_all x1, waiting for transfers between devices, on_device(): lax.all_to_all(sectioned, ('rows', 'cols'), split_axis=2, concat_axis=0,...  6.5 us
    unnamed x2, waiting for transfers between devices  5.12 us
    psum x1, blocking collectives, scan_columns(): selected = lax.psum(partial_value, 'sub')  2.49 us
    all_gather x1, blocking collectives, widen(): lax.all_gather(latent_half, 'sub', axis=2, tiled=True)  2.03 us
    all_gather x1, blocking collectives, widen(): lax.all_gather(scale_shift, 'sub', axis=1, tiled=True)  1.98 us
  transfers between devices with their start and end apart: 2, of which 2 were waited for; matrix products, arithmetic and copies ran while one was open for 0% of the time, Pallas kernels for 0%

commit v1 on v0

--- a/solution.py
+++ b/solution.py
@@ -1,9 +1,13 @@
+import functools
 import math
 
 import jax
 import jax.numpy as jnp
 from jax import lax
+from jax.experimental import pallas as pl
+from jax.experimental.pallas import tpu as pltpu
 from jax.sharding import PartitionSpec as P
+
 
 NS = 16
 RANK = 48
@@ -113,7 +117,7 @@
     return (scanned * jax.nn.silu(seq_gate)).astype(jnp.bfloat16)
 
 
-def on_device(
+def exchange_device(
     latents,
     timestep,
     scan_order,
@@ -177,6 +181,280 @@
     return blended.astype(jnp.bfloat16)
 
 
+LANES = 128
+TOKEN_LIMIT = 256
+LOG2_E = math.log2(math.e)
+
+
+def swap_cores(tensor):
+    return lax.ppermute(tensor, "sub", [(0, 1), (1, 0)])
+
+
+def silu(values):
+    half = 0.5 * values
+    return half + half * jnp.tanh(half)
+
+
+def softplus(values):
+    return jnp.maximum(values, 0.0) + jnp.log(1.0 + jnp.exp(-jnp.abs(values)))
+
+
+def matmul(left, right):
+    return jnp.dot(left, right, preferred_element_type=jnp.float32)
+
+
+def rounded(values):
+    return values.astype(jnp.bfloat16).astype(jnp.float32)
+
+
+def pack_kernel(sel_ref, step_ref, mod_ref, conv_ref, bias_ref, stepb_ref, skip_ref, decay_ref, narrow_ref, wide_ref):
+    coefs, rank, taps = sel_ref.shape[0], step_ref.shape[0], conv_ref.shape[0]
+    half = mod_ref.shape[-1]
+    narrow_ref[:coefs] = sel_ref[...]
+    narrow_ref[coefs : coefs + rank] = step_ref[...]
+    narrow_ref[coefs + rank :, :half] = mod_ref[0]
+    narrow_ref[coefs + rank :, half:] = mod_ref[1]
+    wide_ref[:taps] = conv_ref[...]
+    for i, ref in enumerate((bias_ref, stepb_ref, skip_ref, skip_ref)):
+        wide_ref[taps + i : taps + i + 1] = ref[...]
+    wide_ref[taps + 4 :] = -LOG2_E * jnp.exp(decay_ref[...])
+
+
+def prepare_kernel(lead, order_ref, embed_ref, mod_ref, narrow_ref, pick_ref, live_ref, rows_ref):
+    height = order_ref.shape[0]
+    tokens = pick_ref.shape[0]
+    width, half = tokens // height, mod_ref.shape[-1]
+    own_row = lax.axis_index("rows") * lax.axis_size("cols") + lax.axis_index("cols")
+    position = jnp.int32(0)
+    for k in range(height):
+        position = jnp.where(order_ref[k] == own_row, k, position)
+    slot = lax.broadcasted_iota(jnp.int32, (width, tokens), 0)
+    column = lax.broadcasted_iota(jnp.int32, (width, tokens), 1)
+    picks = []
+    for j in range(height):
+        block = order_ref[jnp.maximum(position - j, 0)] ^ own_row
+        target = jnp.where(position >= j, block * width, -width) + slot
+        picks.append(jnp.where(column == target, 1.0, 0.0))
+        live_ref[j * width : (j + 1) * width] = jnp.full((width, LANES), jnp.where(position >= j, 1.0, 0.0))
+    pick_ref[...] = jnp.concatenate(picks, axis=0).astype(jnp.bfloat16)
+    embed = jnp.broadcast_to(embed_ref[...], (16, embed_ref.shape[1]))
+    weights = (mod_ref[0], mod_ref[1], narrow_ref[lead:, :half], narrow_ref[lead:, half:], mod_ref[2])
+    for i, weight in enumerate(weights):
+        row = rounded(matmul(embed, weight))[:1]
+        rows_ref[i : i + 1] = 1.0 + row if i in (0, 2) else row
+
+
+def block_kernel(
+    taps,
+    states,
+    rank,
+    pick_ref,
+    live_ref,
+    rows_ref,
+    mine_ref,
+    other_ref,
+    in_mine,
+    in_other,
+    narrow_mine,
+    narrow_other,
+    wide_mine,
+    wide_other,
+    out_mine,
+    out_other,
+    result_ref,
+    act_ref,
+    pre_ref,
+    weight_ref,
+):
+    height, width, half = mine_ref.shape
+    tokens = height * width
+    inner = in_mine.shape[-1]
+    core = lax.axis_index("sub")
+    on_first = core == 0
+    coefs = rank + 2 * states
+    scale_mine, shift_mine, scale_other, shift_other, gate_row = [rows_ref[i : i + 1] for i in range(5)]
+
+    pick = pick_ref[...]
+    first = matmul(pick, mine_ref[...].reshape(tokens, half))
+    second = matmul(pick, other_ref[...].reshape(tokens, half))
+    total = jnp.sum(first * first + second * second, axis=-1, keepdims=True)
+    scaling = lax.rsqrt(total / (2.0 * half) + EPSILON)
+    live = live_ref[...]
+    live_half = jnp.concatenate([live] * (half // LANES), axis=1)
+    first = (first * scaling * scale_mine + shift_mine) * live_half
+    second = (second * scaling * scale_other + shift_other) * live_half
+    low = jnp.where(on_first, first, second)
+    high = jnp.where(on_first, second, first)
+    normed = jnp.concatenate([low, high], axis=1).astype(jnp.bfloat16)
+    own_normed = normed[:width]
+
+    sides = ((in_mine, narrow_mine, wide_mine, out_mine), (in_other, narrow_other, wide_other, out_other))
+    selected = None
+    for side, (in_ref, narrow, wide, _) in enumerate(sides):
+        seq = rounded(matmul(normed, in_ref[0]))
+        pieces = []
+        for j in range(height):
+            mixed = wide[taps : taps + 1, :]
+            for back in range(min(taps, height - j)):
+                tap = taps - 1 - back
+                mixed = mixed + wide[tap : tap + 1, :] * seq[(j + back) * width : (j + back + 1) * width]
+            pieces.append(silu(mixed))
+        act = jnp.concatenate(pieces, axis=0).astype(jnp.bfloat16)
+        act_ref[side] = act.astype(jnp.float32)
+        part = lax.dot_general(
+            act, narrow[:coefs, :], (((1,), (1,)), ((), ())), preferred_element_type=jnp.float32
+        )
+        selected = part if selected is None else selected + part
+
+    low_rank = selected[:, :rank].astype(jnp.bfloat16)
+    for side, (_, narrow, _, _) in enumerate(sides):
+        pre_ref[side] = matmul(low_rank, narrow[coefs : coefs + rank, :])
+    own_exit = selected[:width, rank + states :]
+    for j in range(height):
+        product = selected[j * width : (j + 1) * width, rank : rank + states] * own_exit
+        for n in range(states):
+            weight_ref[j, n] = jnp.broadcast_to(product[:, n : n + 1], (width, LANES))
+
+    update = None
+    columns = pl.ds(pl.multiple_of(core * half, LANES), half)
+    for side, (in_ref, _, wide, out_ref) in enumerate(sides):
+        gate = silu(rounded(matmul(own_normed, in_ref[1])))
+        rates = wide[taps + 4 :, :]
+        step_bias, skip = wide[taps + 1 : taps + 2, :], wide[taps + 2 : taps + 3, :]
+        outs = []
+        for block in range(inner // LANES):
+            lanes = slice(block * LANES, (block + 1) * LANES)
+            size = softplus(pre_ref[side, :, lanes] + step_bias[:, lanes])
+            act = act_ref[side, :, lanes]
+            drive = size * act * live
+            rate = [jnp.broadcast_to(rates[n : n + 1, lanes], (width, LANES)) for n in range(states)]
+            scanned = skip[:, lanes] * act[:width]
+            elapsed = None
+            for j in range(height):
+                rows = slice(j * width, (j + 1) * width)
+                mixed = None
+                for n in range(states):
+                    term = weight_ref[j, n]
+                    if j:
+                        term = jnp.exp2(elapsed * rate[n]) * term
+                    mixed = term if mixed is None else mixed + term
+                scanned = scanned + drive[rows] * mixed
+                elapsed = size[rows] if elapsed is None else elapsed + size[rows]
+            outs.append((scanned * gate[:, lanes]).astype(jnp.bfloat16))
+        part = matmul(jnp.concatenate(outs, axis=1), out_ref[:, columns])
+        update = part if update is None else update + part
+    own_latent = mine_ref[0].astype(jnp.float32)
+    result_ref[...] = (own_latent + gate_row * rounded(update)).astype(jnp.bfloat16)
+
+
+def gather_device(
+    latents,
+    timestep,
+    scan_order,
+    modulation,
+    input_proj,
+    conv_weight,
+    conv_bias,
+    select_proj,
+    step_proj,
+    step_bias,
+    decay_log,
+    skip_gain,
+    output_proj,
+):
+    _, width, half = latents.shape
+    lines = lax.axis_size(("rows", "cols"))
+    inner, states = input_proj.shape[-1], decay_log.shape[0]
+    taps, rank = conv_weight.shape[0], step_proj.shape[0]
+    tokens = lines * width
+    freq_count = modulation.shape[0]
+    vmem = pl.BlockSpec(memory_space=pltpu.VMEM)
+    smem = pl.BlockSpec(memory_space=pltpu.SMEM)
+    by_row = modulation.transpose(1, 0, 2)
+    coefs = select_proj.shape[1]
+    packed = pl.pallas_call(
+        pack_kernel,
+        out_shape=(
+            jax.ShapeDtypeStruct((coefs + rank + freq_count, inner), jnp.bfloat16),
+            jax.ShapeDtypeStruct((taps + 4 + states, inner), jnp.float32),
+        ),
+        in_specs=[vmem] * 8,
+        out_specs=(vmem, vmem),
+        compiler_params=pltpu.CompilerParams(vmem_limit_bytes=8 << 20),
+        name="pack_small",
+    )
+    gathered = latents
+    reach = 1
+    model = input_proj.shape[0]
+    cut = model // 3 * 2 if model % 3 == 0 else model // 2
+    parts = [input_proj[part].transpose(1, 0, 2) for part in (slice(0, cut), slice(cut, None))]
+    into = jnp.concatenate(parts, axis=1)
+    out_other = swap_cores(output_proj)
+    while reach < lines:
+        pairs = [(i, i ^ reach) for i in range(lines)]
+        arrived = lax.ppermute(gathered, ("rows", "cols"), pairs)
+        gathered = jnp.concatenate([gathered, arrived], 0)
+        reach = 2 * reach
+    other = swap_cores(gathered)
+    into_other = swap_cores(into)
+    narrow, wide = packed(
+        select_proj.T, step_proj, by_row, conv_weight, conv_bias[None], step_bias[None], skip_gain[None], decay_log
+    )
+    narrow_other = swap_cores(narrow)
+    wide_other = swap_cores(wide)
+    embed = embed_time(timestep, freq_count)
+    pick, live, rows = pl.pallas_call(
+        functools.partial(prepare_kernel, coefs + rank),
+        out_shape=(
+            jax.ShapeDtypeStruct((tokens, tokens), jnp.bfloat16),
+            jax.ShapeDtypeStruct((tokens, LANES), jnp.float32),
+            jax.ShapeDtypeStruct((8, half), jnp.float32),
+        ),
+        in_specs=[smem, vmem, vmem, vmem],
+        out_specs=(vmem, vmem, vmem),
+        compiler_params=pltpu.CompilerParams(vmem_limit_bytes=8 << 20),
+        name="prepare",
+    )(scan_order, embed[None], by_row, narrow_other)
+    operands = (
+        pick,
+        live,
+        rows,
+        gathered,
+        other,
+        into,
+        into_other,
+        narrow,
+        narrow_other,
+        wide,
+        wide_other,
+        output_proj,
+        out_other,
+    )
+    result = pl.pallas_call(
+        functools.partial(block_kernel, taps, states, rank),
+        out_shape=jax.ShapeDtypeStruct((width, half), jnp.bfloat16),
+        in_specs=[vmem] * len(operands),
+        out_specs=vmem,
+        scratch_shapes=[
+            pltpu.VMEM((2, tokens, inner), jnp.float32),
+            pltpu.VMEM((2, tokens, inner), jnp.float32),
+            pltpu.VMEM((lines, states, width, LANES), jnp.float32),
+        ],
+        compiler_params=pltpu.CompilerParams(vmem_limit_bytes=16 << 20),
+        name="scan_block",
+    )(*operands)
+    return result[None]
+
+
+def on_device(latents, *others):
+    rows_dev, grid_width, half = latents.shape
+    lines = lax.axis_size(("rows", "cols"))
+    small = rows_dev == 1 and lines & (lines - 1) == 0 and lines * grid_width <= TOKEN_LIMIT
+    tiled = grid_width % 8 == 0 and half % LANES == 0 and lax.axis_size("sub") == 2
+    run = gather_device if small and tiled else exchange_device
+    return run(latents, *others)
+
+
 def solution(mesh):
     placed = (
         P(("groups", "rows", "cols"), None, "sub"),

time: 61.2 us -> 20.7 us (0.34)
  blocking collectives: 15.4 us -> 0 us
  between operations: 14.6 us -> 0.87 us
  waiting for transfers between devices: 11.6 us -> 4.02 us
  local copies, waits for them, and re-layouts: 7.41 us -> 2.37 us
  Pallas kernels: 0 us -> 3.65 us
  other arithmetic: 2.95 us -> 0.3 us
  starting transfers between devices: 7.17 us -> 9.31 us
  matrix products: 1.65 us -> 0 us
    ppermute x0 -> x8, starting transfers between devices: none -> 9.31 us  [the longest x3 7.69 us: gather_device(): arrived = lax.ppermute(gathered, ('rows', 'cols'), pairs)]
    all_to_all x1 -> x0, blocking collectives: 8.92 us -> none  [on_device(): lax.all_to_all(placed.reshape(line_groups, rows_dev, 1, item_count, inner...]
    all_to_all x1 -> x0, starting transfers between devices: 7.13 us -> none  [on_device(): lax.all_to_all(sectioned, ('rows', 'cols'), split_axis=2, concat_axis=0,...]
    all_to_all x1 -> x0, waiting for transfers between devices: 6.5 us -> none  [on_device(): lax.all_to_all(sectioned, ('rows', 'cols'), split_axis=2, concat_axis=0,...]
    unnamed x31 -> x27, local copies, waits for them, and re-layouts: 6.87 us -> 0.78 us
    unnamed x2 -> x0, waiting for transfers between devices: 5.12 us -> none
    ppermute x0 -> x8, waiting for transfers between devices: none -> 4.02 us  [the longest x3 3.62 us: gather_device(): arrived = lax.ppermute(gathered, ('rows', 'cols'), pairs)]
    all_gather x2 -> x0, blocking collectives: 4.01 us -> none  [the longest x1 2.03 us: widen(): lax.all_gather(latent_half, 'sub', axis=2, tiled=True)]
  transfers between devices with their start and end apart: 2 -> 8, of which waited for: 2 -> 4; matrix products, arithmetic and copies ran while one was open for 0% -> 1% of each run, Pallas kernels for 0% -> 4%
where the time goes in v1:
time: 20.7 us; the launch traced here: 20.5 us
  starting transfers between devices  9.31 us (45%)
  waiting for transfers between devices  4.02 us (19%)
  Pallas kernels  3.65 us (18%)
  local copies, waits for them, and re-layouts  2.37 us (11%)
  between operations  0.87 us (4%)
  other arithmetic  0.3 us (1%)
    ppermute x3, starting transfers between devices, gather_device(): arrived = lax.ppermute(gathered, ('rows', 'cols'), pairs)  7.69 us
    ppermute x3, waiting for transfers between devices, gather_device(): arrived = lax.ppermute(gathered, ('rows', 'cols'), pairs)  3.62 us
    pallas_call x1, Pallas kernels, gather_device(): pl.pallas_call(functools.partial(block_kernel, taps, states, rank), out_s...  2.87 us
    ppermute x5, starting transfers between devices, swap_cores(): return lax.ppermute(tensor, 'sub', [(0, 1), (1, 0)])  1.63 us
    slice x4, local copies, waits for them, and re-layouts, gather_device(): input_proj[part].transpose(1, 0, 2)  1.57 us
    unnamed x27, local copies, waits for them, and re-layouts  0.78 us
    pallas_call x1, Pallas kernels, gather_device(): pl.pallas_call(functools.partial(prepare_kernel, coefs + rank), out_shape...  0.73 us
  transfers between devices with their start and end apart: 8, of which 4 were waited for; matrix products, arithmetic and copies ran while one was open for 1% of the time, Pallas kernels for 4%

profile of v1, /device:TPU:0, one launch (start us, length us, event | category | flops | bytes accessed | tf_op | source)
XLA Modules:
  0.0 20.5 jit_solution(1348950746027399855)
XLA Ops:
  0.0 1.1 %slice-done = bf16[256,2,768]{2,1,0:T(2,128)(2,1)S(1)} async-done(((bf16[768,2,768]{2,1,0:T(2,128)(2,1)}), bf16[256,2,768]{2,1,0:T(2,128)(2,1)S(1)}, s32[]{:S(2)}) %slice-start) | async-done | bytes 786456 | tf_op jit(solution)/shard_map/slice | solution.py:390
  1.1 0.1 copy.21
  1.2 0.4 %slice-done.1 = bf16[512,2,768]{2,1,0:T(2,128)(2,1)S(1)} async-done(((bf16[768,2,768]{2,1,0:T(2,128)(2,1)}), bf16[512,2,768]{2,1,0:T(2,128)(2,1)S(1)}, s32[]{:S(2)}) %slice-start.1) | async-done | bytes 1572888 | tf_op jit(solution)/shard_map/slice | solution.py:390
  1.7 0.2 copy.20
  1.9 0.0 copy-start.1
  1.9 0.0 copy-start.7
  1.9 0.0 copy-start.8
  1.9 0.0 copy-start.9
  1.9 0.0 copy-start.10
  1.9 0.0 copy-start
  1.9 0.0 copy-start.2
  1.9 0.0 copy-start.3
  2.0 0.0 copy-start.4
  2.0 0.0 copy-start.5
  2.0 0.2 pad_maximum_fusion.in_mine
  2.1 0.6 %collective-permute-start.5 = (bf16[2,768,768]{2,1,0:T(8,128)(2,1)S(1)}, bf16[2,768,768]{2,1,0:T(8,128)(2,1)S(1)}, u32[]{:S(2)}, u32[]{:S(2)}) collective-permute-start(bf16[2,768,768]{2,1,0:T(8,128)(2,1)S(1)} %pad_maximum_fusion.in_mine), channel_id=1, source_target_pairs={{0,1},{1,0},{2,3},{3,2},{4,5},{5,4},{6,7},{7,6},{8,9},{9,8},{10,11... | collective-permute-start | bytes 7077896 | tf_op jit(solution)/shard_map/ppermute | solution.py:190
  2.7 0.4 %copy-done.1 = bf16[768,768]{1,0:T(8,128)(2,1)S(1)} copy-done((bf16[768,768]{1,0:T(8,128)(2,1)S(1)}, bf16[768,768]{1,0:T(8,128)(2,1)}, u32[]{:S(2)}) %copy-start.1) | copy-done | bytes 1179672
  3.1 0.5 %collective-permute-start.7 = (bf16[768,768]{1,0:T(8,128)(2,1)S(1)}, bf16[768,768]{1,0:T(8,128)(2,1)S(1)}, u32[]{:S(2)}, u32[]{:S(2)}) collective-permute-start(bf16[768,768]{1,0:T(8,128)(2,1)S(1)} %copy-done.1), channel_id=1, source_target_pairs={{0,1},{1,0},{2,3},{3,2},{4,5},{5,4},{6,7},{7,6},{8,9},{9,8},{10,11... | collective-permute-start | bytes 3538952 | tf_op jit(solution)/shard_map/ppermute | solution.py:190
  3.6 2.5 %collective-permute-start.1 = (bf16[1,8,384]{2,1,0:T(8,128)(2,1)S(1)}, bf16[1,8,384]{2,1,0:T(8,128)(2,1)S(1)}, u32[]{:S(2)}, u32[]{:S(2)}) collective-permute-start(bf16[1,8,384]{2,1,0:T(8,128)(2,1)S(1)} %copy-done.7), channel_id=1, source_target_pairs={{0,2},{2,0},{4,6},{6,4},{8,10},{10,8},{12,14},{14,12},{1,3},{3,1},... | collective-permute-start | bytes 18440 | tf_op jit(solution)/shard_map/ppermute | solution.py:395
  6.2 0.1 pack_small.1
  6.3 0.3 %collective-permute-start.6 = (f32[24,768]{1,0:T(8,128)S(1)}, f32[24,768]{1,0:T(8,128)S(1)}, u32[]{:S(2)}, u32[]{:S(2)}) collective-permute-start(f32[24,768]{1,0:T(8,128)S(1)} %get-tuple-element.14.wide_mine), channel_id=1, source_target_pairs={{0,1},{1,0},{2,3},{3,2},{4,5},{5,4},{6,7},{7,6},{8,9},{9,8},{10,11... | collective-permute-start | bytes 221192 | tf_op jit(solution)/shard_map/ppermute | solution.py:190
  6.6 0.3 %collective-permute-start = (bf16[256,768]{1,0:T(8,128)(2,1)S(1)}, bf16[256,768]{1,0:T(8,128)(2,1)S(1)}, u32[]{:S(2)}, u32[]{:S(2)}) collective-permute-start(bf16[256,768]{1,0:T(8,128)(2,1)S(1)} %get-tuple-element.10.narrow_mine), channel_id=1, source_target_pairs={{0,1},{1,0},{2,3},{3,2},{4,5},{5,4},{6,7},{7,6},{8,9},{9,8},{10,11... | collective-permute-start | bytes 1179656 | tf_op jit(solution)/shard_map/ppermute | solution.py:190
  7.5 0.1 convert_bitcast_fusion
  7.6 0.2 collective-permute-done.1
  7.7 2.1 %collective-permute-start.2 = (bf16[2,8,384]{2,1,0:T(8,128)(2,1)S(1)}, bf16[2,8,384]{2,1,0:T(8,128)(2,1)S(1)}, u32[]{:S(2)}, u32[]{:S(2)}) collective-permute-start(bf16[2,8,384]{2,1,0:T(8,128)(2,1)S(1)} %pad_maximum_fusion.2), channel_id=1, source_target_pairs={{0,4},{2,6},{4,0},{6,2},{8,12},{10,14},{12,8},{14,10},{1,5},{3,7},... | collective-permute-start | bytes 36872 | tf_op jit(solution)/shard_map/ppermute | solution.py:395
  9.8 1.7 %collective-permute-done.2 = bf16[2,8,384]{2,1,0:T(8,128)(2,1)S(1)} collective-permute-done((bf16[2,8,384]{2,1,0:T(8,128)(2,1)S(1)}, bf16[2,8,384]{2,1,0:T(8,128)(2,1)S(1)}, u32[]{:S(2)}, u32[]{:S(2)}) %collective-permute-start.2) | collective-permute-done | bytes 12320 | tf_op jit(solution)/shard_map/ppermute | solution.py:395
  11.5 3.1 %collective-permute-start.3 = (bf16[4,8,384]{2,1,0:T(8,128)(2,1)S(1)}, bf16[4,8,384]{2,1,0:T(8,128)(2,1)S(1)}, u32[]{:S(2)}, u32[]{:S(2)}) collective-permute-start(bf16[4,8,384]{2,1,0:T(8,128)(2,1)S(1)} %pad_maximum_fusion.1), channel_id=1, source_target_pairs={{0,8},{2,10},{4,12},{6,14},{8,0},{10,2},{12,4},{14,6},{1,9},{3,11}... | collective-permute-start | bytes 73736 | tf_op jit(solution)/shard_map/ppermute | solution.py:395
  14.6 1.8 %collective-permute-done.3 = bf16[4,8,384]{2,1,0:T(8,128)(2,1)S(1)} collective-permute-done((bf16[4,8,384]{2,1,0:T(8,128)(2,1)S(1)}, bf16[4,8,384]{2,1,0:T(8,128)(2,1)S(1)}, u32[]{:S(2)}, u32[]{:S(2)}) %collective-permute-start.3) | collective-permute-done | bytes 24608 | tf_op jit(solution)/shard_map/ppermute | solution.py:395
  16.4 0.1 pad_maximum_fusion.3.embed_ref
  16.5 0.7 %prepare.1 = (bf16[64,64]{1,0:T(8,128)(2,1)S(1)}, f32[64,128]{1,0:T(8,128)S(1)}, f32[8,384]{1,0:T(8,128)S(1)}) custom-call(s32[8]{0:T(128)S(1)} %copy-done.6, bf16[1,128]{1,0:T(2,128)(2,1)S(1)} %pad_maximum_fusion.3.embed_ref, bf16[3,128,384]{2,1,0:T(8,128)(2,1)S(1)} %bitcast.15, bf16[256,768]{1,0:T(8,128)(2,1)S(1)} %collective-permute-done.narrow_ref.narrow_other), custom_call_target="tpu_custom_call" | custom-call | tf_op jit(solution)/shard_map/prepare/pallas_call | solution.py:406
  17.3 0.4 %collective-permute-done.4.other_ref = bf16[8,8,384]{2,1,0:T(8,128)(2,1)S(1)} collective-permute-done((bf16[8,8,384]{2,1,0:T(8,128)(2,1)S(1)}, bf16[8,8,384]{2,1,0:T(8,128)(2,1)S(1)}, u32[]{:S(2)}, u32[]{:S(2)}) %collective-permute-start.4) | collective-permute-done | bytes 49184 | tf_op jit(solution)/shard_map/ppermute | solution.py:190
  17.7 2.9 %scan_block.1 = bf16[8,384]{1,0:T(8,128)(2,1)} custom-call(bf16[64,64]{1,0:T(8,128)(2,1)S(1)} %get-tuple-element.11.pick_ref, f32[64,128]{1,0:T(8,128)S(1)} %get-tuple-element.12.live_ref, f32[8,384]{1,0:T(8,128)S(1)} %get-tuple-element.13.rows_ref, bf16[8,8,384]{2,1,0:T(8,128)(2,1)S(1)} %constant_dynamic-update-slice_fusion.mine_ref, ...), custom_call_target="tpu_custom_call" | custom-call | tf_op jit(solution)/shard_map/scan_block/pallas_call | solution.py:433
  (27 shorter events, 0.1 us)
Async XLA Ops:
  0.0 1.1 %slice-start = ((bf16[768,2,768]{2,1,0:T(2,128)(2,1)}), bf16[256,2,768]{2,1,0:T(2,128)(2,1)S(1)}, s32[]{:S(2)}) async-start(bf16[768,2,768]{2,1,0:T(2,128)(2,1)} %param.17), calls=%async_computation | async-start | bytes 1572864 | tf_op jit(solution)/shard_map/slice | solution.py:390
  0.0 1.7 %slice-start.1 = ((bf16[768,2,768]{2,1,0:T(2,128)(2,1)}), bf16[512,2,768]{2,1,0:T(2,128)(2,1)S(1)}, s32[]{:S(2)}) async-start(bf16[768,2,768]{2,1,0:T(2,128)(2,1)} %param.17), calls=%async_computation.1 | async-start | bytes 3145728 | tf_op jit(solution)/shard_map/slice | solution.py:390
  1.9 1.3 %copy-start.1 = (bf16[768,768]{1,0:T(8,128)(2,1)S(1)}, bf16[768,768]{1,0:T(8,128)(2,1)}, u32[]{:S(2)}) copy-start(bf16[768,768]{1,0:T(8,128)(2,1)} %out_mine.1) | copy-start | bytes 3538948
  1.9 1.8 %copy-start.7 = (bf16[1,8,384]{2,1,0:T(8,128)(2,1)S(1)}, bf16[1,8,384]{2,1,0:T(8,128)(2,1)}, u32[]{:S(2)}) copy-start(bf16[1,8,384]{2,1,0:T(8,128)(2,1)} %param.13) | copy-start | bytes 18436
  1.9 4.2 %copy-start.8 = (f32[768]{0:T(1024)S(1)}, f32[768]{0:T(1024)}, u32[]{:S(2)}) copy-start(f32[768]{0:T(1024)} %param.19) | copy-start | bytes 9220
  1.9 4.2 %copy-start.9 = (f32[768]{0:T(1024)S(1)}, f32[768]{0:T(1024)}, u32[]{:S(2)}) copy-start(f32[768]{0:T(1024)} %param.22) | copy-start | bytes 9220
  1.9 4.2 %copy-start.10 = (f32[768]{0:T(1024)S(1)}, f32[768]{0:T(1024)}, u32[]{:S(2)}) copy-start(f32[768]{0:T(1024)} %param.24) | copy-start | bytes 9220
  1.9 4.2 %copy-start = (bf16[128,3,384]{2,0,1:T(8,128)(2,1)S(1)}, bf16[128,3,384]{2,0,1:T(8,128)(2,1)}, u32[]{:S(2)}) copy-start(bf16[128,3,384]{2,0,1:T(8,128)(2,1)} %param.16) | copy-start | bytes 884740
  1.9 4.2 %copy-start.2 = (bf16[768,80]{0,1:T(8,128)(2,1)S(1)}, bf16[768,80]{0,1:T(8,128)(2,1)}, u32[]{:S(2)}) copy-start(bf16[768,80]{0,1:T(8,128)(2,1)} %param.20) | copy-start | bytes 368644
  1.9 4.2 %copy-start.3 = (bf16[48,768]{1,0:T(8,128)(2,1)S(1)}, bf16[48,768]{1,0:T(8,128)(2,1)}, u32[]{:S(2)}) copy-start(bf16[48,768]{1,0:T(8,128)(2,1)} %step_ref.1) | copy-start | bytes 221188
  2.0 4.2 %copy-start.4 = (f32[16,768]{1,0:T(8,128)S(1)}, f32[16,768]{1,0:T(8,128)}, u32[]{:S(2)}) copy-start(f32[16,768]{1,0:T(8,128)} %decay_ref.1) | copy-start | bytes 147460
  2.0 4.2 %copy-start.5 = (f32[4,768]{1,0:T(4,128)S(1)}, f32[4,768]{1,0:T(4,128)}, u32[]{:S(2)}) copy-start(f32[4,768]{1,0:T(4,128)} %conv_ref.1) | copy-start | bytes 36868
  2.0 14.5 %copy-start.6 = (s32[8]{0:T(128)S(1)}, s32[8]{0:T(128)}, u32[]{:S(2)}) copy-start(s32[8]{0:T(128)} %order_ref.1) | copy-start | bytes 100
  2.1 15.5 %collective-permute-start.5 = (bf16[2,768,768]{2,1,0:T(8,128)(2,1)S(1)}, bf16[2,768,768]{2,1,0:T(8,128)(2,1)S(1)}, u32[]{:S(2)}, u32[]{:S(2)}) collective-permute-start(bf16[2,768,768]{2,1,0:T(8,128)(2,1)S(1)} %pad_maximum_fusion.in_mine), channel_id=1, source_target_pairs={{0,1},{1,0},{2,3},{3,2},{4,5},{5,4},{6,7},{7,6},{8,9},{9,8},{10,11... | collective-permute-start | bytes 7077896 | tf_op jit(solution)/shard_map/ppermute | solution.py:190
  3.1 14.5 %collective-permute-start.7 = (bf16[768,768]{1,0:T(8,128)(2,1)S(1)}, bf16[768,768]{1,0:T(8,128)(2,1)S(1)}, u32[]{:S(2)}, u32[]{:S(2)}) collective-permute-start(bf16[768,768]{1,0:T(8,128)(2,1)S(1)} %copy-done.1), channel_id=1, source_target_pairs={{0,1},{1,0},{2,3},{3,2},{4,5},{5,4},{6,7},{7,6},{8,9},{9,8},{10,11... | collective-permute-start | bytes 3538952 | tf_op jit(solution)/shard_map/ppermute | solution.py:190
  3.6 4.1 %collective-permute-start.1 = (bf16[1,8,384]{2,1,0:T(8,128)(2,1)S(1)}, bf16[1,8,384]{2,1,0:T(8,128)(2,1)S(1)}, u32[]{:S(2)}, u32[]{:S(2)}) collective-permute-start(bf16[1,8,384]{2,1,0:T(8,128)(2,1)S(1)} %copy-done.7), channel_id=1, source_target_pairs={{0,2},{2,0},{4,6},{6,4},{8,10},{10,8},{12,14},{14,12},{1,3},{3,1},... | collective-permute-start | bytes 18440 | tf_op jit(solution)/shard_map/ppermute | solution.py:395
  6.3 11.0 %collective-permute-start.6 = (f32[24,768]{1,0:T(8,128)S(1)}, f32[24,768]{1,0:T(8,128)S(1)}, u32[]{:S(2)}, u32[]{:S(2)}) collective-permute-start(f32[24,768]{1,0:T(8,128)S(1)} %get-tuple-element.14.wide_mine), channel_id=1, source_target_pairs={{0,1},{1,0},{2,3},{3,2},{4,5},{5,4},{6,7},{7,6},{8,9},{9,8},{10,11... | collective-permute-start | bytes 221192 | tf_op jit(solution)/shard_map/ppermute | solution.py:190
  6.6 10.0 %collective-permute-start = (bf16[256,768]{1,0:T(8,128)(2,1)S(1)}, bf16[256,768]{1,0:T(8,128)(2,1)S(1)}, u32[]{:S(2)}, u32[]{:S(2)}) collective-permute-start(bf16[256,768]{1,0:T(8,128)(2,1)S(1)} %get-tuple-element.10.narrow_mine), channel_id=1, source_target_pairs={{0,1},{1,0},{2,3},{3,2},{4,5},{5,4},{6,7},{7,6},{8,9},{9,8},{10,11... | collective-permute-start | bytes 1179656 | tf_op jit(solution)/shard_map/ppermute | solution.py:190
  7.7 3.8 %collective-permute-start.2 = (bf16[2,8,384]{2,1,0:T(8,128)(2,1)S(1)}, bf16[2,8,384]{2,1,0:T(8,128)(2,1)S(1)}, u32[]{:S(2)}, u32[]{:S(2)}) collective-permute-start(bf16[2,8,384]{2,1,0:T(8,128)(2,1)S(1)} %pad_maximum_fusion.2), channel_id=1, source_target_pairs={{0,4},{2,6},{4,0},{6,2},{8,12},{10,14},{12,8},{14,10},{1,5},{3,7},... | collective-permute-start | bytes 36872 | tf_op jit(solution)/shard_map/ppermute | solution.py:395
  11.5 4.9 %collective-permute-start.3 = (bf16[4,8,384]{2,1,0:T(8,128)(2,1)S(1)}, bf16[4,8,384]{2,1,0:T(8,128)(2,1)S(1)}, u32[]{:S(2)}, u32[]{:S(2)}) collective-permute-start(bf16[4,8,384]{2,1,0:T(8,128)(2,1)S(1)} %pad_maximum_fusion.1), channel_id=1, source_target_pairs={{0,8},{2,10},{4,12},{6,14},{8,0},{10,2},{12,4},{14,6},{1,9},{3,11}... | collective-permute-start | bytes 73736 | tf_op jit(solution)/shard_map/ppermute | solution.py:395
  16.4 1.2 %collective-permute-start.4 = (bf16[8,8,384]{2,1,0:T(8,128)(2,1)S(1)}, bf16[8,8,384]{2,1,0:T(8,128)(2,1)S(1)}, u32[]{:S(2)}, u32[]{:S(2)}) collective-permute-start(bf16[8,8,384]{2,1,0:T(8,128)(2,1)S(1)} %constant_dynamic-update-slice_fusion.mine_ref), channel_id=1, source_target_pairs={{0,1},{1,0},{2,3},{3,2},{4,5},{5,4},{6,7},{7,6},{8,9},{9,8},{10,11... | collective-permute-start | bytes 147464 | tf_op jit(solution)/shard_map/ppermute | solution.py:190

commit v2 on v1

--- a/solution.py
+++ b/solution.py
@@ -207,41 +207,94 @@
     return values.astype(jnp.bfloat16).astype(jnp.float32)
 
 
-def pack_kernel(sel_ref, step_ref, mod_ref, conv_ref, bias_ref, stepb_ref, skip_ref, decay_ref, narrow_ref, wide_ref):
+def fetch_kernel(
+    sel_ref,
+    step_ref,
+    mod_ref,
+    into_ref,
+    conv_ref,
+    decay_ref,
+    bias_ref,
+    stepb_ref,
+    skip_ref,
+    latent_ref,
+    out_ref,
+    narrow_ref,
+    wide_ref,
+    held_ref,
+    own_ref,
+    send_ref,
+    conv_buf,
+    decay_buf,
+    vector_bufs,
+    sems,
+):
     coefs, rank, taps = sel_ref.shape[0], step_ref.shape[0], conv_ref.shape[0]
     half = mod_ref.shape[-1]
-    narrow_ref[:coefs] = sel_ref[...]
-    narrow_ref[coefs : coefs + rank] = step_ref[...]
-    narrow_ref[coefs + rank :, :half] = mod_ref[0]
-    narrow_ref[coefs + rank :, half:] = mod_ref[1]
-    wide_ref[:taps] = conv_ref[...]
-    for i, ref in enumerate((bias_ref, stepb_ref, skip_ref, skip_ref)):
-        wide_ref[taps + i : taps + i + 1] = ref[...]
-    wide_ref[taps + 4 :] = -LOG2_E * jnp.exp(decay_ref[...])
-
-
-def prepare_kernel(lead, order_ref, embed_ref, mod_ref, narrow_ref, pick_ref, live_ref, rows_ref):
-    height = order_ref.shape[0]
-    tokens = pick_ref.shape[0]
+    vectors = (bias_ref, stepb_ref, skip_ref)
+    moves = [
+        (conv_ref, conv_buf),
+        (decay_ref, decay_buf),
+        *((ref, vector_bufs[i]) for i, ref in enumerate(vectors)),
+        (sel_ref, narrow_ref.at[:coefs]),
+        (step_ref, narrow_ref.at[coefs : coefs + rank]),
+        (mod_ref.at[0], narrow_ref.at[coefs + rank :, :half]),
+        (mod_ref.at[1], narrow_ref.at[coefs + rank :, half:]),
+        (latent_ref, own_ref),
+        (out_ref.at[:, pl.ds(pl.multiple_of((1 - lax.axis_index("sub")) * half, LANES), half)], send_ref),
+        (into_ref.at[: held_ref.shape[0]], held_ref),
+    ]
+    copies = [pltpu.make_async_copy(src, dst, sems.at[i]) for i, (src, dst) in enumerate(moves)]
+    for copy in copies:
+        copy.start()
+    for copy in copies[: 2 + len(vectors)]:
+        copy.wait()
+    wide_ref[:taps] = conv_buf[...]
+    for i, buf in enumerate(vector_bufs):
+        wide_ref[taps + i : taps + i + 1] = buf[...].reshape(1, buf.shape[0])
+    wide_ref[taps + 3 : taps + 4] = jnp.zeros((1, wide_ref.shape[1]), jnp.float32)
+    wide_ref[taps + 4 :] = -LOG2_E * jnp.exp(decay_buf[...])
+    for copy in copies[2 + len(vectors) :]:
+        copy.wait()
+
+
+def prepare_kernel(lead, order_ref, frequency_ref, mod_ref, narrow_ref, pick_ref, live_ref, rows_ref):
+    height = order_ref.shape[0] - 1
+    tokens = pick_ref.shape[1]
     width, half = tokens // height, mod_ref.shape[-1]
     own_row = lax.axis_index("rows") * lax.axis_size("cols") + lax.axis_index("cols")
     position = jnp.int32(0)
     for k in range(height):
         position = jnp.where(order_ref[k] == own_row, k, position)
-    slot = lax.broadcasted_iota(jnp.int32, (width, tokens), 0)
-    column = lax.broadcasted_iota(jnp.int32, (width, tokens), 1)
-    picks = []
+    core = lax.axis_index("sub")
+    slot = lax.broadcasted_iota(jnp.int32, (width, 2 * tokens), 0)
+    column = lax.broadcasted_iota(jnp.int32, (width, 2 * tokens), 1)
+    halves = ([], [])
     for j in range(height):
         block = order_ref[jnp.maximum(position - j, 0)] ^ own_row
-        target = jnp.where(position >= j, block * width, -width) + slot
-        picks.append(jnp.where(column == target, 1.0, 0.0))
+        side = core
+        for bit in range(height.bit_length() - 1):
+            side = side ^ ((block >> bit) & 1)
+        for part in range(2):
+            start = (block + (side ^ part) * height) * width
+            target = jnp.where(position >= j, start, -width) + slot
+            halves[part].append(jnp.where(column == target, 1.0, 0.0))
         live_ref[j * width : (j + 1) * width] = jnp.full((width, LANES), jnp.where(position >= j, 1.0, 0.0))
-    pick_ref[...] = jnp.concatenate(picks, axis=0).astype(jnp.bfloat16)
-    embed = jnp.broadcast_to(embed_ref[...], (16, embed_ref.shape[1]))
-    weights = (mod_ref[0], mod_ref[1], narrow_ref[lead:, :half], narrow_ref[lead:, half:], mod_ref[2])
-    for i, weight in enumerate(weights):
-        row = rounded(matmul(embed, weight))[:1]
-        rows_ref[i : i + 1] = 1.0 + row if i in (0, 2) else row
+    for part in range(2):
+        pick_ref[part] = jnp.concatenate(halves[part], axis=0).astype(jnp.bfloat16)
+    moment = jnp.full(frequency_ref.shape, order_ref[height]).astype(jnp.float32)
+    angles = jnp.broadcast_to(moment * frequency_ref[...], (16, frequency_ref.shape[1]))
+    embed = jnp.concatenate([jnp.cos(angles), jnp.sin(angles)], axis=1).astype(jnp.bfloat16)
+
+    def mod_row(weight):
+        return rounded(matmul(embed, weight))[:1]
+
+    for i in range(2):
+        mine, other = mod_row(mod_ref[i]), mod_row(narrow_ref[lead:, i * half : (i + 1) * half])
+        for part in range(2):
+            row = jnp.where(core == part, mine, other)
+            rows_ref[2 * i + part : 2 * i + part + 1] = row if i else 1.0 + row
+    rows_ref[4:5] = mod_row(mod_ref[2])
 
 
 def block_kernel(
@@ -270,22 +323,22 @@
     tokens = height * width
     inner = in_mine.shape[-1]
     core = lax.axis_index("sub")
-    on_first = core == 0
     coefs = rank + 2 * states
-    scale_mine, shift_mine, scale_other, shift_other, gate_row = [rows_ref[i : i + 1] for i in range(5)]
-
-    pick = pick_ref[...]
-    first = matmul(pick, mine_ref[...].reshape(tokens, half))
-    second = matmul(pick, other_ref[...].reshape(tokens, half))
-    total = jnp.sum(first * first + second * second, axis=-1, keepdims=True)
+    gate_row = rows_ref[4:5]
+
+    gathered = jnp.concatenate([ref[...].reshape(tokens, half) for ref in (mine_ref, other_ref)], axis=0)
+    halves = [matmul(pick_ref[part], gathered) for part in range(2)]
+    total = jnp.sum(halves[0] * halves[0] + halves[1] * halves[1], axis=-1, keepdims=True)
     scaling = lax.rsqrt(total / (2.0 * half) + EPSILON)
     live = live_ref[...]
     live_half = jnp.concatenate([live] * (half // LANES), axis=1)
-    first = (first * scaling * scale_mine + shift_mine) * live_half
-    second = (second * scaling * scale_other + shift_other) * live_half
-    low = jnp.where(on_first, first, second)
-    high = jnp.where(on_first, second, first)
-    normed = jnp.concatenate([low, high], axis=1).astype(jnp.bfloat16)
+    normed = jnp.concatenate(
+        [
+            (halves[part] * scaling * rows_ref[part : part + 1] + rows_ref[part + 2 : part + 3]) * live_half
+            for part in range(2)
+        ],
+        axis=1,
+    ).astype(jnp.bfloat16)
     own_normed = normed[:width]
 
     sides = ((in_mine, narrow_mine, wide_mine, out_mine), (in_other, narrow_other, wide_other, out_other))
@@ -341,7 +394,7 @@
                 scanned = scanned + drive[rows] * mixed
                 elapsed = size[rows] if elapsed is None else elapsed + size[rows]
             outs.append((scanned * gate[:, lanes]).astype(jnp.bfloat16))
-        part = matmul(jnp.concatenate(outs, axis=1), out_ref[:, columns])
+        part = matmul(jnp.concatenate(outs, axis=1), out_ref[...] if side else out_ref[:, columns])
         update = part if update is None else update + part
     own_latent = mine_ref[0].astype(jnp.float32)
     result_ref[...] = (own_latent + gate_row * rounded(update)).astype(jnp.bfloat16)
@@ -372,41 +425,66 @@
     smem = pl.BlockSpec(memory_space=pltpu.SMEM)
     by_row = modulation.transpose(1, 0, 2)
     coefs = select_proj.shape[1]
-    packed = pl.pallas_call(
-        pack_kernel,
+    cut = input_proj.shape[0] // 3 if input_proj.shape[0] % 3 == 0 else input_proj.shape[0] // 2
+    halfway = freq_count // 2
+    frequency = jnp.exp(-math.log(10000.0) * jnp.arange(halfway, dtype=jnp.float32) / halfway)[None]
+    anywhere = pl.BlockSpec(memory_space=pl.ANY)
+    narrow, wide, held, own, out_send = pl.pallas_call(
+        fetch_kernel,
         out_shape=(
             jax.ShapeDtypeStruct((coefs + rank + freq_count, inner), jnp.bfloat16),
             jax.ShapeDtypeStruct((taps + 4 + states, inner), jnp.float32),
+            jax.ShapeDtypeStruct((cut,) + input_proj.shape[1:], jnp.bfloat16),
+            jax.ShapeDtypeStruct(latents.shape, jnp.bfloat16),
+            jax.ShapeDtypeStruct((inner, half), jnp.bfloat16),
         ),
-        in_specs=[vmem] * 8,
-        out_specs=(vmem, vmem),
+        in_specs=[anywhere] * 11,
+        out_specs=[vmem] * 5,
+        scratch_shapes=[
+            pltpu.VMEM(conv_weight.shape, jnp.float32),
+            pltpu.VMEM(decay_log.shape, jnp.float32),
+            [pltpu.VMEM(conv_bias.shape, jnp.float32)] * 3,
+            pltpu.SemaphoreType.DMA((12,)),
+        ],
         compiler_params=pltpu.CompilerParams(vmem_limit_bytes=8 << 20),
-        name="pack_small",
+        name="fetch",
+    )(
+        *(
+            pltpu.with_memory_space_constraint(tensor, pltpu.HBM)
+            for tensor in (
+                select_proj.T,
+                step_proj,
+                by_row,
+                input_proj,
+                conv_weight,
+                decay_log,
+                conv_bias,
+                step_bias,
+                skip_gain,
+                latents,
+                output_proj,
+            )
+        )
     )
     gathered = latents
-    reach = 1
-    model = input_proj.shape[0]
-    cut = model // 3 * 2 if model % 3 == 0 else model // 2
-    parts = [input_proj[part].transpose(1, 0, 2) for part in (slice(0, cut), slice(cut, None))]
-    into = jnp.concatenate(parts, axis=1)
-    out_other = swap_cores(output_proj)
+    reach, hop = 1, 0
+    out_other = swap_cores(out_send)
     while reach < lines:
-        pairs = [(i, i ^ reach) for i in range(lines)]
-        arrived = lax.ppermute(gathered, ("rows", "cols"), pairs)
-        gathered = jnp.concatenate([gathered, arrived], 0)
-        reach = 2 * reach
+        pairs = [(i, i ^ (2 * reach + 1)) for i in range(2 * lines)]
+        arrived = lax.ppermute(gathered, ("rows", "cols", "sub"), pairs)
+        gathered = jnp.concatenate([gathered if hop else own, arrived], 0)
+        reach, hop = 2 * reach, hop + 1
     other = swap_cores(gathered)
+    rest = input_proj[cut:].transpose(1, 0, 2)
+    into = jnp.concatenate([held.transpose(1, 0, 2), rest], axis=1)
     into_other = swap_cores(into)
-    narrow, wide = packed(
-        select_proj.T, step_proj, by_row, conv_weight, conv_bias[None], step_bias[None], skip_gain[None], decay_log
-    )
     narrow_other = swap_cores(narrow)
     wide_other = swap_cores(wide)
-    embed = embed_time(timestep, freq_count)
+    scalars = jnp.concatenate([scan_order, timestep])
     pick, live, rows = pl.pallas_call(
         functools.partial(prepare_kernel, coefs + rank),
         out_shape=(
-            jax.ShapeDtypeStruct((tokens, tokens), jnp.bfloat16),
+            jax.ShapeDtypeStruct((2, tokens, 2 * tokens), jnp.bfloat16),
             jax.ShapeDtypeStruct((tokens, LANES), jnp.float32),
             jax.ShapeDtypeStruct((8, half), jnp.float32),
         ),
@@ -414,7 +492,7 @@
         out_specs=(vmem, vmem, vmem),
         compiler_params=pltpu.CompilerParams(vmem_limit_bytes=8 << 20),
         name="prepare",
-    )(scan_order, embed[None], by_row, narrow_other)
+    )(scalars, frequency, by_row, narrow_other)
     operands = (
         pick,
         live,

time: 20.7 us -> 20.3 us (0.981)
  Pallas kernels: 3.65 us -> 5.5 us
  starting transfers between devices: 9.31 us -> 8.43 us
  waiting for transfers between devices: 4.02 us -> 3.34 us
  local copies, waits for them, and re-layouts: 2.37 us -> 1.74 us
    pallas_call x1, Pallas kernels: 0.05 us -> 1.71 us  [gather_device(): pl.pallas_call(fetch_kernel, out_shape=(jax.ShapeDtypeStruct((coefs + ran...]
    ppermute x3, starting transfers between devices: 7.69 us -> 6.69 us  [gather_device(): arrived = lax.ppermute(gathered, ('rows', 'cols', 'sub'), pairs)]
    unnamed x27 -> x12, local copies, waits for them, and re-layouts: 0.78 us -> 0.24 us
    ppermute x5, waiting for transfers between devices: 0.4 us -> 0.05 us  [swap_cores(): return lax.ppermute(tensor, 'sub', [(0, 1), (1, 0)])]
    ppermute x3, waiting for transfers between devices: 3.62 us -> 3.28 us  [gather_device(): arrived = lax.ppermute(gathered, ('rows', 'cols', 'sub'), pairs)]
    slice x4 -> x2, local copies, waits for them, and re-layouts: 1.57 us -> 1.41 us  [gather_device(): rest = input_proj[cut:].transpose(1, 0, 2)]
  transfers between devices with their start and end apart: 8 -> 8, of which waited for: 4 -> 2; matrix products, arithmetic and copies ran while one was open for 1% -> 1% of each run, Pallas kernels for 4% -> 4%
where the time goes in v2:
time: 20.3 us; the launch traced here: 20 us
  starting transfers between devices  8.43 us (42%)
  Pallas kernels  5.5 us (27%)
  waiting for transfers between devices  3.34 us (16%)
  local copies, waits for them, and re-layouts  1.74 us (9%)
  between operations  0.76 us (4%)
  other arithmetic  0.26 us (1%)
    ppermute x3, starting transfers between devices, gather_device(): arrived = lax.ppermute(gathered, ('rows', 'cols', 'sub'), pairs)  6.69 us
    ppermute x3, waiting for transfers between devices, gather_device(): arrived = lax.ppermute(gathered, ('rows', 'cols', 'sub'), pairs)  3.28 us
    pallas_call x1, Pallas kernels, gather_device(): pl.pallas_call(functools.partial(block_kernel, taps, states, rank), out_s...  2.94 us
    ppermute x5, starting transfers between devices, swap_cores(): return lax.ppermute(tensor, 'sub', [(0, 1), (1, 0)])  1.73 us
    pallas_call x1, Pallas kernels, gather_device(): pl.pallas_call(fetch_kernel, out_shape=(jax.ShapeDtypeStruct((coefs + ran...  1.71 us
    slice x2, local copies, waits for them, and re-layouts, gather_device(): rest = input_proj[cut:].transpose(1, 0, 2)  1.41 us
    pallas_call x1, Pallas kernels, gather_device(): pl.pallas_call(functools.partial(prepare_kernel, coefs + rank), out_shape...  0.84 us
  transfers between devices with their start and end apart: 8, of which 2 were waited for; matrix products, arithmetic and copies ran while one was open for 1% of the time, Pallas kernels for 4%

profile of v2, /device:TPU:0, one launch (start us, length us, event | category | flops | bytes accessed | tf_op | source)
XLA Modules:
  0.0 20.0 jit_solution(17427464009078683669)
XLA Ops:
  0.0 1.4 %slice-done = bf16[512,2,768]{2,1,0:T(2,128)(2,1)S(1)} async-done(((bf16[768,2,768]{2,1,0:T(2,128)(2,1)}), bf16[512,2,768]{2,1,0:T(2,128)(2,1)S(1)}, s32[]{:S(2)}) %slice-start) | async-done | bytes 1572888 | tf_op jit(solution)/shard_map/slice | solution.py:478
  1.4 0.2 copy.19
  1.6 1.7 %fetch.1 = (bf16[256,768]{1,0:T(8,128)(2,1)S(1)}, f32[24,768]{1,0:T(8,128)S(1)}, bf16[256,2,768]{2,1,0:T(2,128)(2,1)S(1)}, bf16[1,8,384]{2,1,0:T(8,128)(2,1)S(1)}, bf16[768,384]{1,0:T(8,128)(2,1)S(1)}) custom-call(bf16[80,768]{1,0:T(8,128)(2,1)} %bitcast.13, bf16[48,768]{1,0:T(8,128)(2,1)} %step_ref.1, bf16[3,128,384]{2,1,0:T(8,128)(2,1)} %bitcast.9, ...), custom_call_target="tpu_custom_call" | custom-call | tf_op jit(solution)/shard_map/fetch/pallas_call | solution.py:432
  3.3 0.1 copy.20
  3.4 0.0 copy-start.2
  3.4 0.0 copy-start.3
  3.4 0.0 copy-start.1
  3.5 0.0 copy-start
  3.5 0.2 pad_maximum_fusion.in_mine
  3.6 0.6 %collective-permute-start.5 = (bf16[2,768,768]{2,1,0:T(8,128)(2,1)S(1)}, bf16[2,768,768]{2,1,0:T(8,128)(2,1)S(1)}, u32[]{:S(2)}, u32[]{:S(2)}) collective-permute-start(bf16[2,768,768]{2,1,0:T(8,128)(2,1)S(1)} %pad_maximum_fusion.in_mine), channel_id=1, source_target_pairs={{0,1},{1,0},{2,3},{3,2},{4,5},{5,4},{6,7},{7,6},{8,9},{9,8},{10,11... | collective-permute-start | bytes 7077896 | tf_op jit(solution)/shard_map/ppermute | solution.py:190
  4.2 0.0 copy-done.2
  4.2 2.6 %collective-permute-start.1 = (bf16[1,8,384]{2,1,0:T(8,128)(2,1)S(1)}, bf16[1,8,384]{2,1,0:T(8,128)(2,1)S(1)}, u32[]{:S(2)}, u32[]{:S(2)}) collective-permute-start(bf16[1,8,384]{2,1,0:T(8,128)(2,1)S(1)} %copy-done.2), channel_id=1, source_target_pairs={{0,3},{1,2},{2,1},{3,0},{4,7},{5,6},{6,5},{7,4},{8,11},{9,10},{10,... | collective-permute-start | bytes 18440 | tf_op jit(solution)/shard_map/ppermute | solution.py:474
  6.8 0.4 %collective-permute-start.6 = (f32[24,768]{1,0:T(8,128)S(1)}, f32[24,768]{1,0:T(8,128)S(1)}, u32[]{:S(2)}, u32[]{:S(2)}) collective-permute-start(f32[24,768]{1,0:T(8,128)S(1)} %get-tuple-element.19.wide_mine), channel_id=1, source_target_pairs={{0,1},{1,0},{2,3},{3,2},{4,5},{5,4},{6,7},{7,6},{8,9},{9,8},{10,11... | collective-permute-start | bytes 221192 | tf_op jit(solution)/shard_map/ppermute | solution.py:190
  7.2 0.1 collective-permute-start
  7.3 0.4 %collective-permute-start.7 = (bf16[768,384]{1,0:T(8,128)(2,1)S(1)}, bf16[768,384]{1,0:T(8,128)(2,1)S(1)}, u32[]{:S(2)}, u32[]{:S(2)}) collective-permute-start(bf16[768,384]{1,0:T(8,128)(2,1)S(1)} %get-tuple-element.20), channel_id=1, source_target_pairs={{0,1},{1,0},{2,3},{3,2},{4,5},{5,4},{6,7},{7,6},{8,9},{9,8},{10,11... | collective-permute-start | bytes 1769480 | tf_op jit(solution)/shard_map/ppermute | solution.py:190
  8.4 0.0 collective-permute-done.1
  8.4 1.5 %collective-permute-start.2 = (bf16[2,8,384]{2,1,0:T(8,128)(2,1)S(1)}, bf16[2,8,384]{2,1,0:T(8,128)(2,1)S(1)}, u32[]{:S(2)}, u32[]{:S(2)}) collective-permute-start(bf16[2,8,384]{2,1,0:T(8,128)(2,1)S(1)} %pad_maximum_fusion.2), channel_id=1, source_target_pairs={{0,5},{1,4},{2,7},{3,6},{4,1},{5,0},{6,3},{7,2},{8,13},{9,12},{10,... | collective-permute-start | bytes 36872 | tf_op jit(solution)/shard_map/ppermute | solution.py:474
  10.0 1.6 %collective-permute-done.2 = bf16[2,8,384]{2,1,0:T(8,128)(2,1)S(1)} collective-permute-done((bf16[2,8,384]{2,1,0:T(8,128)(2,1)S(1)}, bf16[2,8,384]{2,1,0:T(8,128)(2,1)S(1)}, u32[]{:S(2)}, u32[]{:S(2)}) %collective-permute-start.2) | collective-permute-done | bytes 12320 | tf_op jit(solution)/shard_map/ppermute | solution.py:474
  11.6 2.6 %collective-permute-start.3 = (bf16[4,8,384]{2,1,0:T(8,128)(2,1)S(1)}, bf16[4,8,384]{2,1,0:T(8,128)(2,1)S(1)}, u32[]{:S(2)}, u32[]{:S(2)}) collective-permute-start(bf16[4,8,384]{2,1,0:T(8,128)(2,1)S(1)} %pad_maximum_fusion.1), channel_id=1, source_target_pairs={{0,9},{1,8},{2,11},{3,10},{4,13},{5,12},{6,15},{7,14},{8,1},{9,0},... | collective-permute-start | bytes 73736 | tf_op jit(solution)/shard_map/ppermute | solution.py:474
  14.2 1.6 %collective-permute-done.3 = bf16[4,8,384]{2,1,0:T(8,128)(2,1)S(1)} collective-permute-done((bf16[4,8,384]{2,1,0:T(8,128)(2,1)S(1)}, bf16[4,8,384]{2,1,0:T(8,128)(2,1)S(1)}, u32[]{:S(2)}, u32[]{:S(2)}) %collective-permute-start.3) | collective-permute-done | bytes 24608 | tf_op jit(solution)/shard_map/ppermute | solution.py:474
  15.8 0.2 %collective-permute-start.4 = (bf16[8,8,384]{2,1,0:T(8,128)(2,1)S(1)}, bf16[8,8,384]{2,1,0:T(8,128)(2,1)S(1)}, u32[]{:S(2)}, u32[]{:S(2)}) collective-permute-start(bf16[8,8,384]{2,1,0:T(8,128)(2,1)S(1)} %constant_dynamic-update-slice_fusion.mine_ref), channel_id=1, source_target_pairs={{0,1},{1,0},{2,3},{3,2},{4,5},{5,4},{6,7},{7,6},{8,9},{9,8},{10,11... | collective-permute-start | bytes 147464 | tf_op jit(solution)/shard_map/ppermute | solution.py:190
  16.1 0.0 copy-done.3
  16.1 0.1 pad_add_fusion.order_ref
  16.2 0.0 collective-permute-done.narrow_ref.narrow_other
  16.2 0.0 copy-done.1
  16.2 0.8 %prepare.1 = (bf16[2,64,128]{2,1,0:T(8,128)(2,1)S(1)}, f32[64,128]{1,0:T(8,128)S(1)}, f32[8,384]{1,0:T(8,128)S(1)}) custom-call(s32[9]{0:T(128)S(1)} %pad_add_fusion.order_ref, f32[1,64]{1,0:T(1,128)S(1)} %multiply_exponential_fusion.frequency_ref, bf16[3,128,384]{2,1,0:T(8,128)(2,1)S(1)} %bitcast.10, ...), custom_call_target="tpu_custom_call" | custom-call | tf_op jit(solution)/shard_map/prepare/pallas_call | solution.py:484
  17.0 0.0 collective-permute-done.6.wide_other
  17.0 0.0 collective-permute-done.4.other_ref
  17.1 0.0 collective-permute-done.7.out_other
  17.1 0.0 collective-permute-done.5.in_other
  17.1 0.0 copy-done
  17.1 2.9 %scan_block.1 = bf16[8,384]{1,0:T(8,128)(2,1)} custom-call(bf16[2,64,128]{2,1,0:T(8,128)(2,1)S(1)} %get-tuple-element.14.pick_ref, f32[64,128]{1,0:T(8,128)S(1)} %get-tuple-element.15.live_ref, f32[8,384]{1,0:T(8,128)S(1)} %get-tuple-element.16.rows_ref, bf16[8,8,384]{2,1,0:T(8,128)(2,1)S(1)} %constant_dynamic-update-slice_fusion.mine_ref, ...), custom_call_target="tpu_custom_call" | custom-call | tf_op jit(solution)/shard_map/scan_block/pallas_call | solution.py:511
  (8 shorter events, 0.1 us)
Async XLA Ops:
  0.0 1.4 %slice-start = ((bf16[768,2,768]{2,1,0:T(2,128)(2,1)}), bf16[512,2,768]{2,1,0:T(2,128)(2,1)S(1)}, s32[]{:S(2)}) async-start(bf16[768,2,768]{2,1,0:T(2,128)(2,1)} %into_ref.1), calls=%async_computation | async-start | bytes 3145728 | tf_op jit(solution)/shard_map/slice | solution.py:478
  3.4 0.8 %copy-start.2 = (bf16[1,8,384]{2,1,0:T(8,128)(2,1)S(1)}, bf16[1,8,384]{2,1,0:T(8,128)(2,1)}, u32[]{:S(2)}) copy-start(bf16[1,8,384]{2,1,0:T(8,128)(2,1)} %latent_ref.1) | copy-start | bytes 18436
  3.4 12.6 %copy-start.3 = (s32[8]{0:T(128)S(1)}, s32[8]{0:T(128)}, u32[]{:S(2)}) copy-start(s32[8]{0:T(128)} %param.15) | copy-start | bytes 100
  3.4 12.7 %copy-start.1 = (bf16[128,3,384]{2,0,1:T(8,128)(2,1)S(1)}, bf16[128,3,384]{2,0,1:T(8,128)(2,1)}, u32[]{:S(2)}) copy-start(bf16[128,3,384]{2,0,1:T(8,128)(2,1)} %param.16) | copy-start | bytes 884740
  3.5 13.6 %copy-start = (bf16[768,768]{1,0:T(8,128)(2,1)S(1)}, bf16[768,768]{1,0:T(8,128)(2,1)}, u32[]{:S(2)}) copy-start(bf16[768,768]{1,0:T(8,128)(2,1)} %out_mine.1) | copy-start | bytes 3538948
  3.6 13.4 %collective-permute-start.5 = (bf16[2,768,768]{2,1,0:T(8,128)(2,1)S(1)}, bf16[2,768,768]{2,1,0:T(8,128)(2,1)S(1)}, u32[]{:S(2)}, u32[]{:S(2)}) collective-permute-start(bf16[2,768,768]{2,1,0:T(8,128)(2,1)S(1)} %pad_maximum_fusion.in_mine), channel_id=1, source_target_pairs={{0,1},{1,0},{2,3},{3,2},{4,5},{5,4},{6,7},{7,6},{8,9},{9,8},{10,11... | collective-permute-start | bytes 7077896 | tf_op jit(solution)/shard_map/ppermute | solution.py:190
  4.2 4.2 %collective-permute-start.1 = (bf16[1,8,384]{2,1,0:T(8,128)(2,1)S(1)}, bf16[1,8,384]{2,1,0:T(8,128)(2,1)S(1)}, u32[]{:S(2)}, u32[]{:S(2)}) collective-permute-start(bf16[1,8,384]{2,1,0:T(8,128)(2,1)S(1)} %copy-done.2), channel_id=1, source_target_pairs={{0,3},{1,2},{2,1},{3,0},{4,7},{5,6},{6,5},{7,4},{8,11},{9,10},{10,... | collective-permute-start | bytes 18440 | tf_op jit(solution)/shard_map/ppermute | solution.py:474
  6.8 10.2 %collective-permute-start.6 = (f32[24,768]{1,0:T(8,128)S(1)}, f32[24,768]{1,0:T(8,128)S(1)}, u32[]{:S(2)}, u32[]{:S(2)}) collective-permute-start(f32[24,768]{1,0:T(8,128)S(1)} %get-tuple-element.19.wide_mine), channel_id=1, source_target_pairs={{0,1},{1,0},{2,3},{3,2},{4,5},{5,4},{6,7},{7,6},{8,9},{9,8},{10,11... | collective-permute-start | bytes 221192 | tf_op jit(solution)/shard_map/ppermute | solution.py:190
  7.2 9.0 %collective-permute-start = (bf16[256,768]{1,0:T(8,128)(2,1)S(1)}, bf16[256,768]{1,0:T(8,128)(2,1)S(1)}, u32[]{:S(2)}, u32[]{:S(2)}) collective-permute-start(bf16[256,768]{1,0:T(8,128)(2,1)S(1)} %get-tuple-element.13.narrow_mine), channel_id=1, source_target_pairs={{0,1},{1,0},{2,3},{3,2},{4,5},{5,4},{6,7},{7,6},{8,9},{9,8},{10,11... | collective-permute-start | bytes 1179656 | tf_op jit(solution)/shard_map/ppermute | solution.py:190
  7.3 9.8 %collective-permute-start.7 = (bf16[768,384]{1,0:T(8,128)(2,1)S(1)}, bf16[768,384]{1,0:T(8,128)(2,1)S(1)}, u32[]{:S(2)}, u32[]{:S(2)}) collective-permute-start(bf16[768,384]{1,0:T(8,128)(2,1)S(1)} %get-tuple-element.20), channel_id=1, source_target_pairs={{0,1},{1,0},{2,3},{3,2},{4,5},{5,4},{6,7},{7,6},{8,9},{9,8},{10,11... | collective-permute-start | bytes 1769480 | tf_op jit(solution)/shard_map/ppermute | solution.py:190
  8.4 3.2 %collective-permute-start.2 = (bf16[2,8,384]{2,1,0:T(8,128)(2,1)S(1)}, bf16[2,8,384]{2,1,0:T(8,128)(2,1)S(1)}, u32[]{:S(2)}, u32[]{:S(2)}) collective-permute-start(bf16[2,8,384]{2,1,0:T(8,128)(2,1)S(1)} %pad_maximum_fusion.2), channel_id=1, source_target_pairs={{0,5},{1,4},{2,7},{3,6},{4,1},{5,0},{6,3},{7,2},{8,13},{9,12},{10,... | collective-permute-start | bytes 36872 | tf_op jit(solution)/shard_map/ppermute | solution.py:474
  11.6 4.2 %collective-permute-start.3 = (bf16[4,8,384]{2,1,0:T(8,128)(2,1)S(1)}, bf16[4,8,384]{2,1,0:T(8,128)(2,1)S(1)}, u32[]{:S(2)}, u32[]{:S(2)}) collective-permute-start(bf16[4,8,384]{2,1,0:T(8,128)(2,1)S(1)} %pad_maximum_fusion.1), channel_id=1, source_target_pairs={{0,9},{1,8},{2,11},{3,10},{4,13},{5,12},{6,15},{7,14},{8,1},{9,0},... | collective-permute-start | bytes 73736 | tf_op jit(solution)/shard_map/ppermute | solution.py:474
  15.8 1.2 %collective-permute-start.4 = (bf16[8,8,384]{2,1,0:T(8,128)(2,1)S(1)}, bf16[8,8,384]{2,1,0:T(8,128)(2,1)S(1)}, u32[]{:S(2)}, u32[]{:S(2)}) collective-permute-start(bf16[8,8,384]{2,1,0:T(8,128)(2,1)S(1)} %constant_dynamic-update-slice_fusion.mine_ref), channel_id=1, source_target_pairs={{0,1},{1,0},{2,3},{3,2},{4,5},{5,4},{6,7},{7,6},{8,9},{9,8},{10,11... | collective-permute-start | bytes 147464 | tf_op jit(solution)/shard_map/ppermute | solution.py:190

commit v3 on v2

--- a/solution.py
+++ b/solution.py
@@ -183,7 +183,13 @@
 
 LANES = 128
 TOKEN_LIMIT = 256
+STRIDE = 2
 LOG2_E = math.log2(math.e)
+
+
+def hops(lines):
+    count = lines.bit_length() - 1
+    return [1 << i for i in sorted(range(count), key=lambda i: (i != count - 1, i))]
 
 
 def swap_cores(tensor):
@@ -271,10 +277,11 @@
     column = lax.broadcasted_iota(jnp.int32, (width, 2 * tokens), 1)
     halves = ([], [])
     for j in range(height):
-        block = order_ref[jnp.maximum(position - j, 0)] ^ own_row
-        side = core
-        for bit in range(height.bit_length() - 1):
-            side = side ^ ((block >> bit) & 1)
+        away = order_ref[jnp.maximum(position - j, 0)] ^ own_row
+        side, block = core, jnp.int32(0)
+        for hop, reach in enumerate(hops(height)):
+            crossed = (away // reach) & 1
+            side, block = side ^ crossed, block + (crossed << hop)
         for part in range(2):
             start = (block + (side ^ part) * height) * width
             target = jnp.where(position >= j, start, -width) + slot
@@ -318,6 +325,9 @@
     act_ref,
     pre_ref,
     weight_ref,
+    gate_ref,
+    product_ref,
+    latest_ref,
 ):
     height, width, half = mine_ref.shape
     tokens = height * width
@@ -331,6 +341,7 @@
     total = jnp.sum(halves[0] * halves[0] + halves[1] * halves[1], axis=-1, keepdims=True)
     scaling = lax.rsqrt(total / (2.0 * half) + EPSILON)
     live = live_ref[...]
+    visited = jnp.sum(live[:, :1]) / width
     live_half = jnp.concatenate([live] * (half // LANES), axis=1)
     normed = jnp.concatenate(
         [
@@ -343,8 +354,11 @@
 
     sides = ((in_mine, narrow_mine, wide_mine, out_mine), (in_other, narrow_other, wide_other, out_other))
     selected = None
-    for side, (in_ref, narrow, wide, _) in enumerate(sides):
-        seq = rounded(matmul(normed, in_ref[0]))
+    sequences = [rounded(matmul(normed, in_ref[0])) for in_ref, _, _, _ in sides]
+    for side, (in_ref, _, _, _) in enumerate(sides):
+        gate_ref[side] = silu(rounded(matmul(own_normed, in_ref[1])))
+    for side, (_, narrow, wide, _) in enumerate(sides):
+        seq = sequences[side]
         pieces = []
         for j in range(height):
             mixed = wide[taps : taps + 1, :]
@@ -363,41 +377,50 @@
     for side, (_, narrow, _, _) in enumerate(sides):
         pre_ref[side] = matmul(low_rank, narrow[coefs : coefs + rank, :])
     own_exit = selected[:width, rank + states :]
-    for j in range(height):
-        product = selected[j * width : (j + 1) * width, rank : rank + states] * own_exit
-        for n in range(states):
-            weight_ref[j, n] = jnp.broadcast_to(product[:, n : n + 1], (width, LANES))
-
-    update = None
-    columns = pl.ds(pl.multiple_of(core * half, LANES), half)
-    for side, (in_ref, _, wide, out_ref) in enumerate(sides):
-        gate = silu(rounded(matmul(own_normed, in_ref[1])))
-        rates = wide[taps + 4 :, :]
-        step_bias, skip = wide[taps + 1 : taps + 2, :], wide[taps + 2 : taps + 3, :]
-        outs = []
-        for block in range(inner // LANES):
-            lanes = slice(block * LANES, (block + 1) * LANES)
-            size = softplus(pre_ref[side, :, lanes] + step_bias[:, lanes])
-            act = act_ref[side, :, lanes]
-            drive = size * act * live
-            rate = [jnp.broadcast_to(rates[n : n + 1, lanes], (width, LANES)) for n in range(states)]
-            scanned = skip[:, lanes] * act[:width]
-            elapsed = None
-            for j in range(height):
-                rows = slice(j * width, (j + 1) * width)
-                mixed = None
-                for n in range(states):
-                    term = weight_ref[j, n]
-                    if j:
-                        term = jnp.exp2(elapsed * rate[n]) * term
-                    mixed = term if mixed is None else mixed + term
-                scanned = scanned + drive[rows] * mixed
-                elapsed = size[rows] if elapsed is None else elapsed + size[rows]
-            outs.append((scanned * gate[:, lanes]).astype(jnp.bfloat16))
-        part = matmul(jnp.concatenate(outs, axis=1), out_ref[...] if side else out_ref[:, columns])
-        update = part if update is None else update + part
-    own_latent = mine_ref[0].astype(jnp.float32)
-    result_ref[...] = (own_latent + gate_row * rounded(update)).astype(jnp.bfloat16)
+    own_product = selected[:width, rank : rank + states] * own_exit
+    latest_ref[...] = jnp.broadcast_to(jnp.sum(own_product, axis=1, keepdims=True), (width, LANES))
+    for j in range(1, height):
+        rows = slice(j * width, (j + 1) * width)
+        product_ref[rows] = selected[rows, rank : rank + states] * own_exit * live[rows, :states]
+
+    def finish(count):
+        for j in range(1, count):
+            product = product_ref[j * width : (j + 1) * width]
+            for n in range(states):
+                weight_ref[j, n] = jnp.broadcast_to(product[:, n : n + 1], (width, LANES))
+        latest = latest_ref[...]
+        update = None
+        columns = pl.ds(pl.multiple_of(core * half, LANES), half)
+        for side, (_, _, wide, out_ref) in enumerate(sides):
+            rates = wide[taps + 4 :, :]
+            step_bias, skip = wide[taps + 1 : taps + 2, :], wide[taps + 2 : taps + 3, :]
+            outs = []
+            for block in range(inner // LANES):
+                lanes = slice(block * LANES, (block + 1) * LANES)
+                size = softplus(pre_ref[side, : count * width, lanes] + step_bias[:, lanes])
+                act = act_ref[side, : count * width, lanes]
+                drive = size * act
+                rate = [jnp.broadcast_to(rates[n : n + 1, lanes], (width, LANES)) for n in range(states)]
+                scanned = skip[:, lanes] * act[:width] + drive[:width] * latest
+                elapsed = size[:width]
+                for j in range(1, count):
+                    rows = slice(j * width, (j + 1) * width)
+                    mixed = None
+                    for n in range(states):
+                        term = jnp.exp2(elapsed * rate[n]) * weight_ref[j, n]
+                        mixed = term if mixed is None else mixed + term
+                    scanned = scanned + drive[rows] * mixed
+                    elapsed = elapsed + size[rows]
+                outs.append((scanned * gate_ref[side, :, lanes]).astype(jnp.bfloat16))
+            part = matmul(jnp.concatenate(outs, axis=1), out_ref[...] if side else out_ref[:, columns])
+            update = part if update is None else update + part
+        own_latent = mine_ref[0].astype(jnp.float32)
+        result_ref[...] = (own_latent + gate_row * rounded(update)).astype(jnp.bfloat16)
+
+    for start in range(0, height, STRIDE):
+        last = start + STRIDE >= height
+        chosen = visited > start if last else (visited > start) & (visited <= start + STRIDE)
+        pl.when(chosen)(functools.partial(finish, height if last else start + STRIDE))
 
 
 def gather_device(
@@ -467,13 +490,11 @@
         )
     )
     gathered = latents
-    reach, hop = 1, 0
     out_other = swap_cores(out_send)
-    while reach < lines:
+    for hop, reach in enumerate(hops(lines)):
         pairs = [(i, i ^ (2 * reach + 1)) for i in range(2 * lines)]
         arrived = lax.ppermute(gathered, ("rows", "cols", "sub"), pairs)
         gathered = jnp.concatenate([gathered if hop else own, arrived], 0)
-        reach, hop = 2 * reach, hop + 1
     other = swap_cores(gathered)
     rest = input_proj[cut:].transpose(1, 0, 2)
     into = jnp.concatenate([held.transpose(1, 0, 2), rest], axis=1)
@@ -517,6 +538,9 @@
             pltpu.VMEM((2, tokens, inner), jnp.float32),
             pltpu.VMEM((2, tokens, inner), jnp.float32),
             pltpu.VMEM((lines, states, width, LANES), jnp.float32),
+            pltpu.VMEM((2, width, inner), jnp.float32),
+            pltpu.VMEM((tokens, states), jnp.float32),
+            pltpu.VMEM((width, LANES), jnp.float32),
         ],
         compiler_params=pltpu.CompilerParams(vmem_limit_bytes=16 << 20),
         name="scan_block",

time: 20.3 us -> 20.7 us (1.020)
  waiting for transfers between devices: 3.34 us -> 3.99 us
  starting transfers between devices: 8.43 us -> 7.96 us
  Pallas kernels: 5.5 us -> 5.78 us
    ppermute x3, waiting for transfers between devices: 3.28 us -> 3.82 us  [gather_device(): arrived = lax.ppermute(gathered, ('rows', 'cols', 'sub'), pairs)]
    ppermute x3, starting transfers between devices: 6.69 us -> 6.36 us  [gather_device(): arrived = lax.ppermute(gathered, ('rows', 'cols', 'sub'), pairs)]
    pallas_call x1, Pallas kernels: 2.94 us -> 3.22 us  [gather_device(): pl.pallas_call(functools.partial(block_kernel, taps, states, rank), out_s...]
  transfers between devices with their start and end apart: 8 -> 8, of which waited for: 2 -> 3; matrix products, arithmetic and copies ran while one was open for 1% -> 1% of each run, Pallas kernels for 4% -> 4%
where the time goes in v3:
time: 20.7 us; the launch traced here: 20.5 us
  starting transfers between devices  7.96 us (38%)
  Pallas kernels  5.78 us (28%)
  waiting for transfers between devices  3.99 us (19%)
  local copies, waits for them, and re-layouts  1.74 us (8%)
  between operations  0.76 us (4%)
  other arithmetic  0.26 us (1%)
    ppermute x3, starting transfers between devices, gather_device(): arrived = lax.ppermute(gathered, ('rows', 'cols', 'sub'), pairs)  6.36 us
    ppermute x3, waiting for transfers between devices, gather_device(): arrived = lax.ppermute(gathered, ('rows', 'cols', 'sub'), pairs)  3.82 us
    pallas_call x1, Pallas kernels, gather_device(): pl.pallas_call(functools.partial(block_kernel, taps, states, rank), out_s...  3.22 us
    pallas_call x1, Pallas kernels, gather_device(): pl.pallas_call(fetch_kernel, out_shape=(jax.ShapeDtypeStruct((coefs + ran...  1.71 us
    ppermute x5, starting transfers between devices, swap_cores(): return lax.ppermute(tensor, 'sub', [(0, 1), (1, 0)])  1.6 us
    slice x2, local copies, waits for them, and re-layouts, gather_device(): rest = input_proj[cut:].transpose(1, 0, 2)  1.41 us
    pallas_call x1, Pallas kernels, gather_device(): pl.pallas_call(functools.partial(prepare_kernel, coefs + rank), out_shape...  0.85 us
  transfers between devices with their start and end apart: 8, of which 3 were waited for; matrix products, arithmetic and copies ran while one was open for 1% of the time, Pallas kernels for 4%

profile of v3, /device:TPU:0, one launch (start us, length us, event | category | flops | bytes accessed | tf_op | source)
XLA Modules:
  0.0 20.5 jit_solution(7962953255908507147)
XLA Ops:
  0.0 1.4 %slice-done = bf16[512,2,768]{2,1,0:T(2,128)(2,1)S(1)} async-done(((bf16[768,2,768]{2,1,0:T(2,128)(2,1)}), bf16[512,2,768]{2,1,0:T(2,128)(2,1)S(1)}, s32[]{:S(2)}) %slice-start) | async-done | bytes 1572888 | tf_op jit(solution)/shard_map/slice | solution.py:499
  1.4 0.2 copy.19
  1.6 1.7 %fetch.1 = (bf16[256,768]{1,0:T(8,128)(2,1)S(1)}, f32[24,768]{1,0:T(8,128)S(1)}, bf16[256,2,768]{2,1,0:T(2,128)(2,1)S(1)}, bf16[1,8,384]{2,1,0:T(8,128)(2,1)S(1)}, bf16[768,384]{1,0:T(8,128)(2,1)S(1)}) custom-call(bf16[80,768]{1,0:T(8,128)(2,1)} %bitcast.13, bf16[48,768]{1,0:T(8,128)(2,1)} %step_ref.1, bf16[3,128,384]{2,1,0:T(8,128)(2,1)} %bitcast.9, ...), custom_call_target="tpu_custom_call" | custom-call | tf_op jit(solution)/shard_map/fetch/pallas_call | solution.py:455
  3.3 0.1 copy.20
  3.4 0.0 copy-start.2
  3.4 0.0 copy-start.3
  3.4 0.0 copy-start.1
  3.5 0.0 copy-start
  3.5 0.2 pad_maximum_fusion.in_mine
  3.6 0.6 %collective-permute-start.5 = (bf16[2,768,768]{2,1,0:T(8,128)(2,1)S(1)}, bf16[2,768,768]{2,1,0:T(8,128)(2,1)S(1)}, u32[]{:S(2)}, u32[]{:S(2)}) collective-permute-start(bf16[2,768,768]{2,1,0:T(8,128)(2,1)S(1)} %pad_maximum_fusion.in_mine), channel_id=1, source_target_pairs={{0,1},{1,0},{2,3},{3,2},{4,5},{5,4},{6,7},{7,6},{8,9},{9,8},{10,11... | collective-permute-start | bytes 7077896 | tf_op jit(solution)/shard_map/ppermute | solution.py:196
  4.2 0.0 copy-done.2
  4.2 3.7 %collective-permute-start.1 = (bf16[1,8,384]{2,1,0:T(8,128)(2,1)S(1)}, bf16[1,8,384]{2,1,0:T(8,128)(2,1)S(1)}, u32[]{:S(2)}, u32[]{:S(2)}) collective-permute-start(bf16[1,8,384]{2,1,0:T(8,128)(2,1)S(1)} %copy-done.2), channel_id=1, source_target_pairs={{0,9},{1,8},{2,11},{3,10},{4,13},{5,12},{6,15},{7,14},{8,1},{9,0},... | collective-permute-start | bytes 18440 | tf_op jit(solution)/shard_map/ppermute | solution.py:496
  7.9 0.4 %collective-permute-start.6 = (f32[24,768]{1,0:T(8,128)S(1)}, f32[24,768]{1,0:T(8,128)S(1)}, u32[]{:S(2)}, u32[]{:S(2)}) collective-permute-start(f32[24,768]{1,0:T(8,128)S(1)} %get-tuple-element.19.wide_mine), channel_id=1, source_target_pairs={{0,1},{1,0},{2,3},{3,2},{4,5},{5,4},{6,7},{7,6},{8,9},{9,8},{10,11... | collective-permute-start | bytes 221192 | tf_op jit(solution)/shard_map/ppermute | solution.py:196
  8.3 0.1 collective-permute-start
  8.4 0.4 %collective-permute-start.7 = (bf16[768,384]{1,0:T(8,128)(2,1)S(1)}, bf16[768,384]{1,0:T(8,128)(2,1)S(1)}, u32[]{:S(2)}, u32[]{:S(2)}) collective-permute-start(bf16[768,384]{1,0:T(8,128)(2,1)S(1)} %get-tuple-element.20), channel_id=1, source_target_pairs={{0,1},{1,0},{2,3},{3,2},{4,5},{5,4},{6,7},{7,6},{8,9},{9,8},{10,11... | collective-permute-start | bytes 1769480 | tf_op jit(solution)/shard_map/ppermute | solution.py:196
  9.5 0.0 collective-permute-done.1
  9.5 1.3 %collective-permute-start.2 = (bf16[2,8,384]{2,1,0:T(8,128)(2,1)S(1)}, bf16[2,8,384]{2,1,0:T(8,128)(2,1)S(1)}, u32[]{:S(2)}, u32[]{:S(2)}) collective-permute-start(bf16[2,8,384]{2,1,0:T(8,128)(2,1)S(1)} %pad_maximum_fusion.2), channel_id=1, source_target_pairs={{0,3},{1,2},{2,1},{3,0},{4,7},{5,6},{6,5},{7,4},{8,11},{9,10},{10,... | collective-permute-start | bytes 36872 | tf_op jit(solution)/shard_map/ppermute | solution.py:496
  10.8 1.9 %collective-permute-done.2 = bf16[2,8,384]{2,1,0:T(8,128)(2,1)S(1)} collective-permute-done((bf16[2,8,384]{2,1,0:T(8,128)(2,1)S(1)}, bf16[2,8,384]{2,1,0:T(8,128)(2,1)S(1)}, u32[]{:S(2)}, u32[]{:S(2)}) %collective-permute-start.2) | collective-permute-done | bytes 12320 | tf_op jit(solution)/shard_map/ppermute | solution.py:496
  12.7 1.4 %collective-permute-start.3 = (bf16[4,8,384]{2,1,0:T(8,128)(2,1)S(1)}, bf16[4,8,384]{2,1,0:T(8,128)(2,1)S(1)}, u32[]{:S(2)}, u32[]{:S(2)}) collective-permute-start(bf16[4,8,384]{2,1,0:T(8,128)(2,1)S(1)} %pad_maximum_fusion.1), channel_id=1, source_target_pairs={{0,5},{1,4},{2,7},{3,6},{4,1},{5,0},{6,3},{7,2},{8,13},{9,12},{10,... | collective-permute-start | bytes 73736 | tf_op jit(solution)/shard_map/ppermute | solution.py:496
  14.1 1.9 %collective-permute-done.3 = bf16[4,8,384]{2,1,0:T(8,128)(2,1)S(1)} collective-permute-done((bf16[4,8,384]{2,1,0:T(8,128)(2,1)S(1)}, bf16[4,8,384]{2,1,0:T(8,128)(2,1)S(1)}, u32[]{:S(2)}, u32[]{:S(2)}) %collective-permute-start.3) | collective-permute-done | bytes 24608 | tf_op jit(solution)/shard_map/ppermute | solution.py:496
  16.0 0.1 collective-permute-start.4
  16.1 0.0 copy-done.3
  16.1 0.1 pad_add_fusion.order_ref
  16.2 0.0 collective-permute-done.narrow_ref.narrow_other
  16.2 0.0 copy-done.1
  16.2 0.8 %prepare.1 = (bf16[2,64,128]{2,1,0:T(8,128)(2,1)S(1)}, f32[64,128]{1,0:T(8,128)S(1)}, f32[8,384]{1,0:T(8,128)S(1)}) custom-call(s32[9]{0:T(128)S(1)} %pad_add_fusion.order_ref, f32[1,64]{1,0:T(1,128)S(1)} %multiply_exponential_fusion.frequency_ref, bf16[3,128,384]{2,1,0:T(8,128)(2,1)S(1)} %bitcast.10, ...), custom_call_target="tpu_custom_call" | custom-call | tf_op jit(solution)/shard_map/prepare/pallas_call | solution.py:505
  17.1 0.0 collective-permute-done.6.wide_other
  17.1 0.2 collective-permute-done.4.other_ref
  17.3 0.0 collective-permute-done.7.out_other
  17.3 0.0 collective-permute-done.5.in_other
  17.3 0.0 copy-done
  17.3 3.2 %scan_block.1 = bf16[8,384]{1,0:T(8,128)(2,1)} custom-call(bf16[2,64,128]{2,1,0:T(8,128)(2,1)S(1)} %get-tuple-element.14.pick_ref, f32[64,128]{1,0:T(8,128)S(1)} %get-tuple-element.15.live_ref, f32[8,384]{1,0:T(8,128)S(1)} %get-tuple-element.16.rows_ref, bf16[8,8,384]{2,1,0:T(8,128)(2,1)S(1)} %constant_dynamic-update-slice_fusion.mine_ref, ...), custom_call_target="tpu_custom_call" | custom-call | tf_op jit(solution)/shard_map/scan_block/pallas_call | solution.py:532
  (8 shorter events, 0.1 us)
Async XLA Ops:
  0.0 1.4 %slice-start = ((bf16[768,2,768]{2,1,0:T(2,128)(2,1)}), bf16[512,2,768]{2,1,0:T(2,128)(2,1)S(1)}, s32[]{:S(2)}) async-start(bf16[768,2,768]{2,1,0:T(2,128)(2,1)} %into_ref.1), calls=%async_computation | async-start | bytes 3145728 | tf_op jit(solution)/shard_map/slice | solution.py:499
  3.4 0.8 %copy-start.2 = (bf16[1,8,384]{2,1,0:T(8,128)(2,1)S(1)}, bf16[1,8,384]{2,1,0:T(8,128)(2,1)}, u32[]{:S(2)}) copy-start(bf16[1,8,384]{2,1,0:T(8,128)(2,1)} %latent_ref.1) | copy-start | bytes 18436
  3.4 12.7 %copy-start.3 = (s32[8]{0:T(128)S(1)}, s32[8]{0:T(128)}, u32[]{:S(2)}) copy-start(s32[8]{0:T(128)} %param.15) | copy-start | bytes 100
  3.4 12.8 %copy-start.1 = (bf16[128,3,384]{2,0,1:T(8,128)(2,1)S(1)}, bf16[128,3,384]{2,0,1:T(8,128)(2,1)}, u32[]{:S(2)}) copy-start(bf16[128,3,384]{2,0,1:T(8,128)(2,1)} %param.16) | copy-start | bytes 884740
  3.5 13.8 %copy-start = (bf16[768,768]{1,0:T(8,128)(2,1)S(1)}, bf16[768,768]{1,0:T(8,128)(2,1)}, u32[]{:S(2)}) copy-start(bf16[768,768]{1,0:T(8,128)(2,1)} %out_mine.1) | copy-start | bytes 3538948
  3.6 13.6 %collective-permute-start.5 = (bf16[2,768,768]{2,1,0:T(8,128)(2,1)S(1)}, bf16[2,768,768]{2,1,0:T(8,128)(2,1)S(1)}, u32[]{:S(2)}, u32[]{:S(2)}) collective-permute-start(bf16[2,768,768]{2,1,0:T(8,128)(2,1)S(1)} %pad_maximum_fusion.in_mine), channel_id=1, source_target_pairs={{0,1},{1,0},{2,3},{3,2},{4,5},{5,4},{6,7},{7,6},{8,9},{9,8},{10,11... | collective-permute-start | bytes 7077896 | tf_op jit(solution)/shard_map/ppermute | solution.py:196
  4.2 5.3 %collective-permute-start.1 = (bf16[1,8,384]{2,1,0:T(8,128)(2,1)S(1)}, bf16[1,8,384]{2,1,0:T(8,128)(2,1)S(1)}, u32[]{:S(2)}, u32[]{:S(2)}) collective-permute-start(bf16[1,8,384]{2,1,0:T(8,128)(2,1)S(1)} %copy-done.2), channel_id=1, source_target_pairs={{0,9},{1,8},{2,11},{3,10},{4,13},{5,12},{6,15},{7,14},{8,1},{9,0},... | collective-permute-start | bytes 18440 | tf_op jit(solution)/shard_map/ppermute | solution.py:496
  7.9 9.2 %collective-permute-start.6 = (f32[24,768]{1,0:T(8,128)S(1)}, f32[24,768]{1,0:T(8,128)S(1)}, u32[]{:S(2)}, u32[]{:S(2)}) collective-permute-start(f32[24,768]{1,0:T(8,128)S(1)} %get-tuple-element.19.wide_mine), channel_id=1, source_target_pairs={{0,1},{1,0},{2,3},{3,2},{4,5},{5,4},{6,7},{7,6},{8,9},{9,8},{10,11... | collective-permute-start | bytes 221192 | tf_op jit(solution)/shard_map/ppermute | solution.py:196
  8.3 7.9 %collective-permute-start = (bf16[256,768]{1,0:T(8,128)(2,1)S(1)}, bf16[256,768]{1,0:T(8,128)(2,1)S(1)}, u32[]{:S(2)}, u32[]{:S(2)}) collective-permute-start(bf16[256,768]{1,0:T(8,128)(2,1)S(1)} %get-tuple-element.13.narrow_mine), channel_id=1, source_target_pairs={{0,1},{1,0},{2,3},{3,2},{4,5},{5,4},{6,7},{7,6},{8,9},{9,8},{10,11... | collective-permute-start | bytes 1179656 | tf_op jit(solution)/shard_map/ppermute | solution.py:196
  8.4 8.9 %collective-permute-start.7 = (bf16[768,384]{1,0:T(8,128)(2,1)S(1)}, bf16[768,384]{1,0:T(8,128)(2,1)S(1)}, u32[]{:S(2)}, u32[]{:S(2)}) collective-permute-start(bf16[768,384]{1,0:T(8,128)(2,1)S(1)} %get-tuple-element.20), channel_id=1, source_target_pairs={{0,1},{1,0},{2,3},{3,2},{4,5},{5,4},{6,7},{7,6},{8,9},{9,8},{10,11... | collective-permute-start | bytes 1769480 | tf_op jit(solution)/shard_map/ppermute | solution.py:196
  9.5 3.2 %collective-permute-start.2 = (bf16[2,8,384]{2,1,0:T(8,128)(2,1)S(1)}, bf16[2,8,384]{2,1,0:T(8,128)(2,1)S(1)}, u32[]{:S(2)}, u32[]{:S(2)}) collective-permute-start(bf16[2,8,384]{2,1,0:T(8,128)(2,1)S(1)} %pad_maximum_fusion.2), channel_id=1, source_target_pairs={{0,3},{1,2},{2,1},{3,0},{4,7},{5,6},{6,5},{7,4},{8,11},{9,10},{10,... | collective-permute-start | bytes 36872 | tf_op jit(solution)/shard_map/ppermute | solution.py:496
  12.7 3.3 %collective-permute-start.3 = (bf16[4,8,384]{2,1,0:T(8,128)(2,1)S(1)}, bf16[4,8,384]{2,1,0:T(8,128)(2,1)S(1)}, u32[]{:S(2)}, u32[]{:S(2)}) collective-permute-start(bf16[4,8,384]{2,1,0:T(8,128)(2,1)S(1)} %pad_maximum_fusion.1), channel_id=1, source_target_pairs={{0,5},{1,4},{2,7},{3,6},{4,1},{5,0},{6,3},{7,2},{8,13},{9,12},{10,... | collective-permute-start | bytes 73736 | tf_op jit(solution)/shard_map/ppermute | solution.py:496
  16.0 1.2 %collective-permute-start.4 = (bf16[8,8,384]{2,1,0:T(8,128)(2,1)S(1)}, bf16[8,8,384]{2,1,0:T(8,128)(2,1)S(1)}, u32[]{:S(2)}, u32[]{:S(2)}) collective-permute-start(bf16[8,8,384]{2,1,0:T(8,128)(2,1)S(1)} %constant_dynamic-update-slice_fusion.mine_ref), channel_id=1, source_target_pairs={{0,1},{1,0},{2,3},{3,2},{4,5},{5,4},{6,7},{7,6},{8,9},{9,8},{10,11... | collective-permute-start | bytes 147464 | tf_op jit(solution)/shard_map/ppermute | solution.py:196

commit v4 on v2

--- a/solution.py
+++ b/solution.py
@@ -184,6 +184,11 @@
 LANES = 128
 TOKEN_LIMIT = 256
 LOG2_E = math.log2(math.e)
+
+
+def hops(lines):
+    count = lines.bit_length() - 1
+    return [1 << i for i in sorted(range(count), key=lambda i: (i != count - 1, i))]
 
 
 def swap_cores(tensor):
@@ -271,10 +276,11 @@
     column = lax.broadcasted_iota(jnp.int32, (width, 2 * tokens), 1)
     halves = ([], [])
     for j in range(height):
-        block = order_ref[jnp.maximum(position - j, 0)] ^ own_row
-        side = core
-        for bit in range(height.bit_length() - 1):
-            side = side ^ ((block >> bit) & 1)
+        away = order_ref[jnp.maximum(position - j, 0)] ^ own_row
+        side, block = core, jnp.int32(0)
+        for hop, reach in enumerate(hops(height)):
+            crossed = (away // reach) & 1
+            side, block = side ^ crossed, block + (crossed << hop)
         for part in range(2):
             start = (block + (side ^ part) * height) * width
             target = jnp.where(position >= j, start, -width) + slot
@@ -363,8 +369,11 @@
     for side, (_, narrow, _, _) in enumerate(sides):
         pre_ref[side] = matmul(low_rank, narrow[coefs : coefs + rank, :])
     own_exit = selected[:width, rank + states :]
-    for j in range(height):
+    own_product = selected[:width, rank : rank + states] * own_exit
+    latest = jnp.broadcast_to(jnp.sum(own_product, axis=1, keepdims=True), (width, LANES))
+    for j in range(1, height):
         product = selected[j * width : (j + 1) * width, rank : rank + states] * own_exit
+        product = product * live[j * width : (j + 1) * width, :states]
         for n in range(states):
             weight_ref[j, n] = jnp.broadcast_to(product[:, n : n + 1], (width, LANES))
 
@@ -379,20 +388,18 @@
             lanes = slice(block * LANES, (block + 1) * LANES)
             size = softplus(pre_ref[side, :, lanes] + step_bias[:, lanes])
             act = act_ref[side, :, lanes]
-            drive = size * act * live
+            drive = size * act
             rate = [jnp.broadcast_to(rates[n : n + 1, lanes], (width, LANES)) for n in range(states)]
-            scanned = skip[:, lanes] * act[:width]
-            elapsed = None
-            for j in range(height):
+            scanned = skip[:, lanes] * act[:width] + drive[:width] * latest
+            elapsed = size[:width]
+            for j in range(1, height):
                 rows = slice(j * width, (j + 1) * width)
                 mixed = None
                 for n in range(states):
-                    term = weight_ref[j, n]
-                    if j:
-                        term = jnp.exp2(elapsed * rate[n]) * term
+                    term = jnp.exp2(elapsed * rate[n]) * weight_ref[j, n]
                     mixed = term if mixed is None else mixed + term
                 scanned = scanned + drive[rows] * mixed
-                elapsed = size[rows] if elapsed is None else elapsed + size[rows]
+                elapsed = elapsed + size[rows]
             outs.append((scanned * gate[:, lanes]).astype(jnp.bfloat16))
         part = matmul(jnp.concatenate(outs, axis=1), out_ref[...] if side else out_ref[:, columns])
         update = part if update is None else update + part
@@ -467,13 +474,11 @@
         )
     )
     gathered = latents
-    reach, hop = 1, 0
     out_other = swap_cores(out_send)
-    while reach < lines:
+    for hop, reach in enumerate(hops(lines)):
         pairs = [(i, i ^ (2 * reach + 1)) for i in range(2 * lines)]
         arrived = lax.ppermute(gathered, ("rows", "cols", "sub"), pairs)
         gathered = jnp.concatenate([gathered if hop else own, arrived], 0)
-        reach, hop = 2 * reach, hop + 1
     other = swap_cores(gathered)
     rest = input_proj[cut:].transpose(1, 0, 2)
     into = jnp.concatenate([held.transpose(1, 0, 2), rest], axis=1)

time: 20.3 us -> 20.5 us (level)
  waiting for transfers between devices: 3.34 us -> 3.99 us
  starting transfers between devices: 8.43 us -> 7.96 us
    ppermute x3, waiting for transfers between devices: 3.28 us -> 3.82 us  [gather_device(): arrived = lax.ppermute(gathered, ('rows', 'cols', 'sub'), pairs)]
    ppermute x3, starting transfers between devices: 6.69 us -> 6.36 us  [gather_device(): arrived = lax.ppermute(gathered, ('rows', 'cols', 'sub'), pairs)]
  transfers between devices with their start and end apart: 8 -> 8, of which waited for: 2 -> 3; matrix products, arithmetic and copies ran while one was open for 1% -> 1% of each run, Pallas kernels for 4% -> 4%
where the time goes in v4:
time: 20.5 us; the launch traced here: 20.2 us
  starting transfers between devices  7.96 us (39%)
  Pallas kernels  5.51 us (27%)
  waiting for transfers between devices  3.99 us (19%)
  local copies, waits for them, and re-layouts  1.74 us (8%)
  between operations  0.76 us (4%)
  other arithmetic  0.26 us (1%)
    ppermute x3, starting transfers between devices, gather_device(): arrived = lax.ppermute(gathered, ('rows', 'cols', 'sub'), pairs)  6.36 us
    ppermute x3, waiting for transfers between devices, gather_device(): arrived = lax.ppermute(gathered, ('rows', 'cols', 'sub'), pairs)  3.82 us
    pallas_call x1, Pallas kernels, gather_device(): pl.pallas_call(functools.partial(block_kernel, taps, states, rank), out_s...  2.96 us
    pallas_call x1, Pallas kernels, gather_device(): pl.pallas_call(fetch_kernel, out_shape=(jax.ShapeDtypeStruct((coefs + ran...  1.71 us
    ppermute x5, starting transfers between devices, swap_cores(): return lax.ppermute(tensor, 'sub', [(0, 1), (1, 0)])  1.6 us
    slice x2, local copies, waits for them, and re-layouts, gather_device(): rest = input_proj[cut:].transpose(1, 0, 2)  1.41 us
    pallas_call x1, Pallas kernels, gather_device(): pl.pallas_call(functools.partial(prepare_kernel, coefs + rank), out_shape...  0.85 us
  transfers between devices with their start and end apart: 8, of which 3 were waited for; matrix products, arithmetic and copies ran while one was open for 1% of the time, Pallas kernels for 4%

profile of v4, /device:TPU:0, one launch (start us, length us, event | category | flops | bytes accessed | tf_op | source)
XLA Modules:
  0.0 20.2 jit_solution(2108105666464148164)
XLA Ops:
  0.0 1.4 %slice-done = bf16[512,2,768]{2,1,0:T(2,128)(2,1)S(1)} async-done(((bf16[768,2,768]{2,1,0:T(2,128)(2,1)}), bf16[512,2,768]{2,1,0:T(2,128)(2,1)S(1)}, s32[]{:S(2)}) %slice-start) | async-done | bytes 1572888 | tf_op jit(solution)/shard_map/slice | solution.py:483
  1.4 0.2 copy.19
  1.6 1.7 %fetch.1 = (bf16[256,768]{1,0:T(8,128)(2,1)S(1)}, f32[24,768]{1,0:T(8,128)S(1)}, bf16[256,2,768]{2,1,0:T(2,128)(2,1)S(1)}, bf16[1,8,384]{2,1,0:T(8,128)(2,1)S(1)}, bf16[768,384]{1,0:T(8,128)(2,1)S(1)}) custom-call(bf16[80,768]{1,0:T(8,128)(2,1)} %bitcast.13, bf16[48,768]{1,0:T(8,128)(2,1)} %step_ref.1, bf16[3,128,384]{2,1,0:T(8,128)(2,1)} %bitcast.9, ...), custom_call_target="tpu_custom_call" | custom-call | tf_op jit(solution)/shard_map/fetch/pallas_call | solution.py:439
  3.3 0.1 copy.20
  3.4 0.0 copy-start.2
  3.4 0.0 copy-start.3
  3.4 0.0 copy-start.1
  3.5 0.0 copy-start
  3.5 0.2 pad_maximum_fusion.in_mine
  3.6 0.6 %collective-permute-start.5 = (bf16[2,768,768]{2,1,0:T(8,128)(2,1)S(1)}, bf16[2,768,768]{2,1,0:T(8,128)(2,1)S(1)}, u32[]{:S(2)}, u32[]{:S(2)}) collective-permute-start(bf16[2,768,768]{2,1,0:T(8,128)(2,1)S(1)} %pad_maximum_fusion.in_mine), channel_id=1, source_target_pairs={{0,1},{1,0},{2,3},{3,2},{4,5},{5,4},{6,7},{7,6},{8,9},{9,8},{10,11... | collective-permute-start | bytes 7077896 | tf_op jit(solution)/shard_map/ppermute | solution.py:195
  4.2 0.0 copy-done.2
  4.2 3.7 %collective-permute-start.1 = (bf16[1,8,384]{2,1,0:T(8,128)(2,1)S(1)}, bf16[1,8,384]{2,1,0:T(8,128)(2,1)S(1)}, u32[]{:S(2)}, u32[]{:S(2)}) collective-permute-start(bf16[1,8,384]{2,1,0:T(8,128)(2,1)S(1)} %copy-done.2), channel_id=1, source_target_pairs={{0,9},{1,8},{2,11},{3,10},{4,13},{5,12},{6,15},{7,14},{8,1},{9,0},... | collective-permute-start | bytes 18440 | tf_op jit(solution)/shard_map/ppermute | solution.py:480
  7.9 0.4 %collective-permute-start.6 = (f32[24,768]{1,0:T(8,128)S(1)}, f32[24,768]{1,0:T(8,128)S(1)}, u32[]{:S(2)}, u32[]{:S(2)}) collective-permute-start(f32[24,768]{1,0:T(8,128)S(1)} %get-tuple-element.19.wide_mine), channel_id=1, source_target_pairs={{0,1},{1,0},{2,3},{3,2},{4,5},{5,4},{6,7},{7,6},{8,9},{9,8},{10,11... | collective-permute-start | bytes 221192 | tf_op jit(solution)/shard_map/ppermute | solution.py:195
  8.3 0.1 collective-permute-start
  8.4 0.4 %collective-permute-start.7 = (bf16[768,384]{1,0:T(8,128)(2,1)S(1)}, bf16[768,384]{1,0:T(8,128)(2,1)S(1)}, u32[]{:S(2)}, u32[]{:S(2)}) collective-permute-start(bf16[768,384]{1,0:T(8,128)(2,1)S(1)} %get-tuple-element.20), channel_id=1, source_target_pairs={{0,1},{1,0},{2,3},{3,2},{4,5},{5,4},{6,7},{7,6},{8,9},{9,8},{10,11... | collective-permute-start | bytes 1769480 | tf_op jit(solution)/shard_map/ppermute | solution.py:195
  9.5 0.0 collective-permute-done.1
  9.5 1.3 %collective-permute-start.2 = (bf16[2,8,384]{2,1,0:T(8,128)(2,1)S(1)}, bf16[2,8,384]{2,1,0:T(8,128)(2,1)S(1)}, u32[]{:S(2)}, u32[]{:S(2)}) collective-permute-start(bf16[2,8,384]{2,1,0:T(8,128)(2,1)S(1)} %pad_maximum_fusion.2), channel_id=1, source_target_pairs={{0,3},{1,2},{2,1},{3,0},{4,7},{5,6},{6,5},{7,4},{8,11},{9,10},{10,... | collective-permute-start | bytes 36872 | tf_op jit(solution)/shard_map/ppermute | solution.py:480
  10.8 1.9 %collective-permute-done.2 = bf16[2,8,384]{2,1,0:T(8,128)(2,1)S(1)} collective-permute-done((bf16[2,8,384]{2,1,0:T(8,128)(2,1)S(1)}, bf16[2,8,384]{2,1,0:T(8,128)(2,1)S(1)}, u32[]{:S(2)}, u32[]{:S(2)}) %collective-permute-start.2) | collective-permute-done | bytes 12320 | tf_op jit(solution)/shard_map/ppermute | solution.py:480
  12.7 1.4 %collective-permute-start.3 = (bf16[4,8,384]{2,1,0:T(8,128)(2,1)S(1)}, bf16[4,8,384]{2,1,0:T(8,128)(2,1)S(1)}, u32[]{:S(2)}, u32[]{:S(2)}) collective-permute-start(bf16[4,8,384]{2,1,0:T(8,128)(2,1)S(1)} %pad_maximum_fusion.1), channel_id=1, source_target_pairs={{0,5},{1,4},{2,7},{3,6},{4,1},{5,0},{6,3},{7,2},{8,13},{9,12},{10,... | collective-permute-start | bytes 73736 | tf_op jit(solution)/shard_map/ppermute | solution.py:480
  14.1 1.9 %collective-permute-done.3 = bf16[4,8,384]{2,1,0:T(8,128)(2,1)S(1)} collective-permute-done((bf16[4,8,384]{2,1,0:T(8,128)(2,1)S(1)}, bf16[4,8,384]{2,1,0:T(8,128)(2,1)S(1)}, u32[]{:S(2)}, u32[]{:S(2)}) %collective-permute-start.3) | collective-permute-done | bytes 24608 | tf_op jit(solution)/shard_map/ppermute | solution.py:480
  16.0 0.1 collective-permute-start.4
  16.1 0.0 copy-done.3
  16.1 0.1 pad_add_fusion.order_ref
  16.2 0.0 collective-permute-done.narrow_ref.narrow_other
  16.2 0.0 copy-done.1
  16.2 0.8 %prepare.1 = (bf16[2,64,128]{2,1,0:T(8,128)(2,1)S(1)}, f32[64,128]{1,0:T(8,128)S(1)}, f32[8,384]{1,0:T(8,128)S(1)}) custom-call(s32[9]{0:T(128)S(1)} %pad_add_fusion.order_ref, f32[1,64]{1,0:T(1,128)S(1)} %multiply_exponential_fusion.frequency_ref, bf16[3,128,384]{2,1,0:T(8,128)(2,1)S(1)} %bitcast.10, ...), custom_call_target="tpu_custom_call" | custom-call | tf_op jit(solution)/shard_map/prepare/pallas_call | solution.py:489
  17.1 0.0 collective-permute-done.6.wide_other
  17.1 0.2 collective-permute-done.4.other_ref
  17.3 0.0 collective-permute-done.7.out_other
  17.3 0.0 collective-permute-done.5.in_other
  17.3 0.0 copy-done
  17.3 3.0 %scan_block.1 = bf16[8,384]{1,0:T(8,128)(2,1)} custom-call(bf16[2,64,128]{2,1,0:T(8,128)(2,1)S(1)} %get-tuple-element.14.pick_ref, f32[64,128]{1,0:T(8,128)S(1)} %get-tuple-element.15.live_ref, f32[8,384]{1,0:T(8,128)S(1)} %get-tuple-element.16.rows_ref, bf16[8,8,384]{2,1,0:T(8,128)(2,1)S(1)} %constant_dynamic-update-slice_fusion.mine_ref, ...), custom_call_target="tpu_custom_call" | custom-call | tf_op jit(solution)/shard_map/scan_block/pallas_call | solution.py:516
  (8 shorter events, 0.1 us)
Async XLA Ops:
  0.0 1.4 %slice-start = ((bf16[768,2,768]{2,1,0:T(2,128)(2,1)}), bf16[512,2,768]{2,1,0:T(2,128)(2,1)S(1)}, s32[]{:S(2)}) async-start(bf16[768,2,768]{2,1,0:T(2,128)(2,1)} %into_ref.1), calls=%async_computation | async-start | bytes 3145728 | tf_op jit(solution)/shard_map/slice | solution.py:483
  3.4 0.8 %copy-start.2 = (bf16[1,8,384]{2,1,0:T(8,128)(2,1)S(1)}, bf16[1,8,384]{2,1,0:T(8,128)(2,1)}, u32[]{:S(2)}) copy-start(bf16[1,8,384]{2,1,0:T(8,128)(2,1)} %latent_ref.1) | copy-start | bytes 18436
  3.4 12.7 %copy-start.3 = (s32[8]{0:T(128)S(1)}, s32[8]{0:T(128)}, u32[]{:S(2)}) copy-start(s32[8]{0:T(128)} %param.15) | copy-start | bytes 100
  3.4 12.8 %copy-start.1 = (bf16[128,3,384]{2,0,1:T(8,128)(2,1)S(1)}, bf16[128,3,384]{2,0,1:T(8,128)(2,1)}, u32[]{:S(2)}) copy-start(bf16[128,3,384]{2,0,1:T(8,128)(2,1)} %param.16) | copy-start | bytes 884740
  3.5 13.8 %copy-start = (bf16[768,768]{1,0:T(8,128)(2,1)S(1)}, bf16[768,768]{1,0:T(8,128)(2,1)}, u32[]{:S(2)}) copy-start(bf16[768,768]{1,0:T(8,128)(2,1)} %out_mine.1) | copy-start | bytes 3538948
  3.6 13.6 %collective-permute-start.5 = (bf16[2,768,768]{2,1,0:T(8,128)(2,1)S(1)}, bf16[2,768,768]{2,1,0:T(8,128)(2,1)S(1)}, u32[]{:S(2)}, u32[]{:S(2)}) collective-permute-start(bf16[2,768,768]{2,1,0:T(8,128)(2,1)S(1)} %pad_maximum_fusion.in_mine), channel_id=1, source_target_pairs={{0,1},{1,0},{2,3},{3,2},{4,5},{5,4},{6,7},{7,6},{8,9},{9,8},{10,11... | collective-permute-start | bytes 7077896 | tf_op jit(solution)/shard_map/ppermute | solution.py:195
  4.2 5.3 %collective-permute-start.1 = (bf16[1,8,384]{2,1,0:T(8,128)(2,1)S(1)}, bf16[1,8,384]{2,1,0:T(8,128)(2,1)S(1)}, u32[]{:S(2)}, u32[]{:S(2)}) collective-permute-start(bf16[1,8,384]{2,1,0:T(8,128)(2,1)S(1)} %copy-done.2), channel_id=1, source_target_pairs={{0,9},{1,8},{2,11},{3,10},{4,13},{5,12},{6,15},{7,14},{8,1},{9,0},... | collective-permute-start | bytes 18440 | tf_op jit(solution)/shard_map/ppermute | solution.py:480
  7.9 9.2 %collective-permute-start.6 = (f32[24,768]{1,0:T(8,128)S(1)}, f32[24,768]{1,0:T(8,128)S(1)}, u32[]{:S(2)}, u32[]{:S(2)}) collective-permute-start(f32[24,768]{1,0:T(8,128)S(1)} %get-tuple-element.19.wide_mine), channel_id=1, source_target_pairs={{0,1},{1,0},{2,3},{3,2},{4,5},{5,4},{6,7},{7,6},{8,9},{9,8},{10,11... | collective-permute-start | bytes 221192 | tf_op jit(solution)/shard_map/ppermute | solution.py:195
  8.3 7.9 %collective-permute-start = (bf16[256,768]{1,0:T(8,128)(2,1)S(1)}, bf16[256,768]{1,0:T(8,128)(2,1)S(1)}, u32[]{:S(2)}, u32[]{:S(2)}) collective-permute-start(bf16[256,768]{1,0:T(8,128)(2,1)S(1)} %get-tuple-element.13.narrow_mine), channel_id=1, source_target_pairs={{0,1},{1,0},{2,3},{3,2},{4,5},{5,4},{6,7},{7,6},{8,9},{9,8},{10,11... | collective-permute-start | bytes 1179656 | tf_op jit(solution)/shard_map/ppermute | solution.py:195
  8.4 8.9 %collective-permute-start.7 = (bf16[768,384]{1,0:T(8,128)(2,1)S(1)}, bf16[768,384]{1,0:T(8,128)(2,1)S(1)}, u32[]{:S(2)}, u32[]{:S(2)}) collective-permute-start(bf16[768,384]{1,0:T(8,128)(2,1)S(1)} %get-tuple-element.20), channel_id=1, source_target_pairs={{0,1},{1,0},{2,3},{3,2},{4,5},{5,4},{6,7},{7,6},{8,9},{9,8},{10,11... | collective-permute-start | bytes 1769480 | tf_op jit(solution)/shard_map/ppermute | solution.py:195
  9.5 3.2 %collective-permute-start.2 = (bf16[2,8,384]{2,1,0:T(8,128)(2,1)S(1)}, bf16[2,8,384]{2,1,0:T(8,128)(2,1)S(1)}, u32[]{:S(2)}, u32[]{:S(2)}) collective-permute-start(bf16[2,8,384]{2,1,0:T(8,128)(2,1)S(1)} %pad_maximum_fusion.2), channel_id=1, source_target_pairs={{0,3},{1,2},{2,1},{3,0},{4,7},{5,6},{6,5},{7,4},{8,11},{9,10},{10,... | collective-permute-start | bytes 36872 | tf_op jit(solution)/shard_map/ppermute | solution.py:480
  12.7 3.3 %collective-permute-start.3 = (bf16[4,8,384]{2,1,0:T(8,128)(2,1)S(1)}, bf16[4,8,384]{2,1,0:T(8,128)(2,1)S(1)}, u32[]{:S(2)}, u32[]{:S(2)}) collective-permute-start(bf16[4,8,384]{2,1,0:T(8,128)(2,1)S(1)} %pad_maximum_fusion.1), channel_id=1, source_target_pairs={{0,5},{1,4},{2,7},{3,6},{4,1},{5,0},{6,3},{7,2},{8,13},{9,12},{10,... | collective-permute-start | bytes 73736 | tf_op jit(solution)/shard_map/ppermute | solution.py:480
  16.0 1.2 %collective-permute-start.4 = (bf16[8,8,384]{2,1,0:T(8,128)(2,1)S(1)}, bf16[8,8,384]{2,1,0:T(8,128)(2,1)S(1)}, u32[]{:S(2)}, u32[]{:S(2)}) collective-permute-start(bf16[8,8,384]{2,1,0:T(8,128)(2,1)S(1)} %constant_dynamic-update-slice_fusion.mine_ref), channel_id=1, source_target_pairs={{0,1},{1,0},{2,3},{3,2},{4,5},{5,4},{6,7},{7,6},{8,9},{9,8},{10,11... | collective-permute-start | bytes 147464 | tf_op jit(solution)/shard_map/ppermute | solution.py:195

commit v5 on v4

--- a/solution.py
+++ b/solution.py
@@ -212,6 +212,33 @@
     return values.astype(jnp.bfloat16).astype(jnp.float32)
 
 
+def choose_rows(order_ref, pick_ref, live_ref):
+    height = order_ref.shape[0]
+    tokens = pick_ref.shape[1]
+    width = tokens // height
+    own_row = lax.axis_index("rows") * lax.axis_size("cols") + lax.axis_index("cols")
+    core = lax.axis_index("sub")
+    position = jnp.int32(0)
+    for k in range(height):
+        position = jnp.where(order_ref[k] == own_row, k, position)
+    slot = lax.broadcasted_iota(jnp.int32, (width, 2 * tokens), 0)
+    column = lax.broadcasted_iota(jnp.int32, (width, 2 * tokens), 1)
+    halves = ([], [])
+    for j in range(height):
+        away = order_ref[jnp.maximum(position - j, 0)] ^ own_row
+        side, block = core, jnp.int32(0)
+        for hop, reach in enumerate(hops(height)):
+            crossed = (away >> (reach.bit_length() - 1)) & 1
+            side, block = side ^ crossed, block + (crossed << hop)
+        for part in range(2):
+            start = (block + (side ^ part) * height) * width
+            target = jnp.where(position >= j, start, -width) + slot
+            halves[part].append(jnp.where(column == target, 1.0, 0.0))
+        live_ref[j * width : (j + 1) * width] = jnp.full((width, LANES), jnp.where(position >= j, 1.0, 0.0))
+    for part in range(2):
+        pick_ref[part] = jnp.concatenate(halves[part], axis=0).astype(jnp.bfloat16)
+
+
 def fetch_kernel(
     sel_ref,
     step_ref,
@@ -224,11 +251,15 @@
     skip_ref,
     latent_ref,
     out_ref,
+    order_ref,
     narrow_ref,
     wide_ref,
     held_ref,
     own_ref,
     send_ref,
+    pick_ref,
+    live_ref,
+    order_buf,
     conv_buf,
     decay_buf,
     vector_bufs,
@@ -238,6 +269,7 @@
     half = mod_ref.shape[-1]
     vectors = (bias_ref, stepb_ref, skip_ref)
     moves = [
+        (order_ref, order_buf),
         (conv_ref, conv_buf),
         (decay_ref, decay_buf),
         *((ref, vector_bufs[i]) for i, ref in enumerate(vectors)),
@@ -252,44 +284,22 @@
     copies = [pltpu.make_async_copy(src, dst, sems.at[i]) for i, (src, dst) in enumerate(moves)]
     for copy in copies:
         copy.start()
-    for copy in copies[: 2 + len(vectors)]:
+    for copy in copies[: 3 + len(vectors)]:
         copy.wait()
     wide_ref[:taps] = conv_buf[...]
     for i, buf in enumerate(vector_bufs):
         wide_ref[taps + i : taps + i + 1] = buf[...].reshape(1, buf.shape[0])
     wide_ref[taps + 3 : taps + 4] = jnp.zeros((1, wide_ref.shape[1]), jnp.float32)
     wide_ref[taps + 4 :] = -LOG2_E * jnp.exp(decay_buf[...])
-    for copy in copies[2 + len(vectors) :]:
+    choose_rows(order_buf, pick_ref, live_ref)
+    for copy in copies[3 + len(vectors) :]:
         copy.wait()
 
 
-def prepare_kernel(lead, order_ref, frequency_ref, mod_ref, narrow_ref, pick_ref, live_ref, rows_ref):
-    height = order_ref.shape[0] - 1
-    tokens = pick_ref.shape[1]
-    width, half = tokens // height, mod_ref.shape[-1]
-    own_row = lax.axis_index("rows") * lax.axis_size("cols") + lax.axis_index("cols")
-    position = jnp.int32(0)
-    for k in range(height):
-        position = jnp.where(order_ref[k] == own_row, k, position)
+def prepare_kernel(lead, angle_ref, mod_ref, narrow_ref, rows_ref):
+    half = mod_ref.shape[-1]
     core = lax.axis_index("sub")
-    slot = lax.broadcasted_iota(jnp.int32, (width, 2 * tokens), 0)
-    column = lax.broadcasted_iota(jnp.int32, (width, 2 * tokens), 1)
-    halves = ([], [])
-    for j in range(height):
-        away = order_ref[jnp.maximum(position - j, 0)] ^ own_row
-        side, block = core, jnp.int32(0)
-        for hop, reach in enumerate(hops(height)):
-            crossed = (away // reach) & 1
-            side, block = side ^ crossed, block + (crossed << hop)
-        for part in range(2):
-            start = (block + (side ^ part) * height) * width
-            target = jnp.where(position >= j, start, -width) + slot
-            halves[part].append(jnp.where(column == target, 1.0, 0.0))
-        live_ref[j * width : (j + 1) * width] = jnp.full((width, LANES), jnp.where(position >= j, 1.0, 0.0))
-    for part in range(2):
-        pick_ref[part] = jnp.concatenate(halves[part], axis=0).astype(jnp.bfloat16)
-    moment = jnp.full(frequency_ref.shape, order_ref[height]).astype(jnp.float32)
-    angles = jnp.broadcast_to(moment * frequency_ref[...], (16, frequency_ref.shape[1]))
+    angles = jnp.broadcast_to(angle_ref[...], (16, angle_ref.shape[1]))
     embed = jnp.concatenate([jnp.cos(angles), jnp.sin(angles)], axis=1).astype(jnp.bfloat16)
 
     def mod_row(weight):
@@ -429,14 +439,11 @@
     tokens = lines * width
     freq_count = modulation.shape[0]
     vmem = pl.BlockSpec(memory_space=pltpu.VMEM)
-    smem = pl.BlockSpec(memory_space=pltpu.SMEM)
     by_row = modulation.transpose(1, 0, 2)
     coefs = select_proj.shape[1]
     cut = input_proj.shape[0] // 3 if input_proj.shape[0] % 3 == 0 else input_proj.shape[0] // 2
-    halfway = freq_count // 2
-    frequency = jnp.exp(-math.log(10000.0) * jnp.arange(halfway, dtype=jnp.float32) / halfway)[None]
     anywhere = pl.BlockSpec(memory_space=pl.ANY)
-    narrow, wide, held, own, out_send = pl.pallas_call(
+    narrow, wide, held, own, out_send, pick, live = pl.pallas_call(
         fetch_kernel,
         out_shape=(
             jax.ShapeDtypeStruct((coefs + rank + freq_count, inner), jnp.bfloat16),
@@ -444,14 +451,17 @@
             jax.ShapeDtypeStruct((cut,) + input_proj.shape[1:], jnp.bfloat16),
             jax.ShapeDtypeStruct(latents.shape, jnp.bfloat16),
             jax.ShapeDtypeStruct((inner, half), jnp.bfloat16),
+            jax.ShapeDtypeStruct((2, tokens, 2 * tokens), jnp.bfloat16),
+            jax.ShapeDtypeStruct((tokens, LANES), jnp.float32),
         ),
-        in_specs=[anywhere] * 11,
-        out_specs=[vmem] * 5,
+        in_specs=[anywhere] * 12,
+        out_specs=[vmem] * 7,
         scratch_shapes=[
+            pltpu.SMEM(scan_order.shape, jnp.int32),
             pltpu.VMEM(conv_weight.shape, jnp.float32),
             pltpu.VMEM(decay_log.shape, jnp.float32),
             [pltpu.VMEM(conv_bias.shape, jnp.float32)] * 3,
-            pltpu.SemaphoreType.DMA((12,)),
+            pltpu.SemaphoreType.DMA((13,)),
         ],
         compiler_params=pltpu.CompilerParams(vmem_limit_bytes=8 << 20),
         name="fetch",
@@ -470,6 +480,7 @@
                 skip_gain,
                 latents,
                 output_proj,
+                scan_order,
             )
         )
     )
@@ -485,19 +496,17 @@
     into_other = swap_cores(into)
     narrow_other = swap_cores(narrow)
     wide_other = swap_cores(wide)
-    scalars = jnp.concatenate([scan_order, timestep])
-    pick, live, rows = pl.pallas_call(
+    halfway = freq_count // 2
+    frequency = jnp.exp(-math.log(10000.0) * jnp.arange(halfway, dtype=jnp.float32) / halfway)
+    angles = timestep.astype(jnp.float32)[:, None] * frequency[None]
+    rows = pl.pallas_call(
         functools.partial(prepare_kernel, coefs + rank),
-        out_shape=(
-            jax.ShapeDtypeStruct((2, tokens, 2 * tokens), jnp.bfloat16),
-            jax.ShapeDtypeStruct((tokens, LANES), jnp.float32),
-            jax.ShapeDtypeStruct((8, half), jnp.float32),
-        ),
-        in_specs=[smem, vmem, vmem, vmem],
-        out_specs=(vmem, vmem, vmem),
+        out_shape=jax.ShapeDtypeStruct((8, half), jnp.float32),
+        in_specs=[vmem, vmem, vmem],
+        out_specs=vmem,
         compiler_params=pltpu.CompilerParams(vmem_limit_bytes=8 << 20),
         name="prepare",
-    )(scalars, frequency, by_row, narrow_other)
+    )(angles, by_row, narrow_other)
     operands = (
         pick,
         live,

time: 20.5 us -> 20.4 us (level)
  waiting for transfers between devices: 3.99 us -> 4.6 us
  Pallas kernels: 5.51 us -> 4.97 us
    ppermute x5, waiting for transfers between devices: 0.17 us -> 0.8 us  [swap_cores(): return lax.ppermute(tensor, 'sub', [(0, 1), (1, 0)])]
    pallas_call x1, Pallas kernels: 0.85 us -> 0.29 us  [gather_device(): pl.pallas_call(functools.partial(prepare_kernel, coefs + rank), out_shape...]
  transfers between devices with their start and end apart: 8 -> 8, of which waited for: 3 -> 3; matrix products, arithmetic and copies ran while one was open for 1% -> 0% of each run, Pallas kernels for 4% -> 1%
where the time goes in v5:
time: 20.4 us; the launch traced here: 20.2 us
  starting transfers between devices  7.98 us (39%)
  Pallas kernels  4.97 us (24%)
  waiting for transfers between devices  4.6 us (23%)
  local copies, waits for them, and re-layouts  1.73 us (8%)
  between operations  0.75 us (4%)
    ppermute x3, starting transfers between devices, gather_device(): arrived = lax.ppermute(gathered, ('rows', 'cols', 'sub'), pairs)  6.37 us
    ppermute x3, waiting for transfers between devices, gather_device(): arrived = lax.ppermute(gathered, ('rows', 'cols', 'sub'), pairs)  3.81 us
    pallas_call x1, Pallas kernels, gather_device(): pl.pallas_call(functools.partial(block_kernel, taps, states, rank), out_s...  2.96 us
    pallas_call x1, Pallas kernels, gather_device(): pl.pallas_call(fetch_kernel, out_shape=(jax.ShapeDtypeStruct((coefs + ran...  1.72 us
    ppermute x5, starting transfers between devices, swap_cores(): return lax.ppermute(tensor, 'sub', [(0, 1), (1, 0)])  1.61 us
    slice x2, local copies, waits for them, and re-layouts, gather_device(): rest = input_proj[cut:].transpose(1, 0, 2)  1.41 us
    ppermute x5, waiting for transfers between devices, swap_cores(): return lax.ppermute(tensor, 'sub', [(0, 1), (1, 0)])  0.8 us
  transfers between devices with their start and end apart: 8, of which 3 were waited for; matrix products, arithmetic and copies ran while one was open for 0% of the time, Pallas kernels for 1%

profile of v5, /device:TPU:0, one launch (start us, length us, event | category | flops | bytes accessed | tf_op | source)
XLA Modules:
  0.0 20.2 jit_solution(16110508734348139153)
XLA Ops:
  0.0 0.0 slice-start
  0.0 1.4 %slice-done = bf16[512,2,768]{2,1,0:T(2,128)(2,1)S(1)} async-done(((bf16[768,2,768]{2,1,0:T(2,128)(2,1)}), bf16[512,2,768]{2,1,0:T(2,128)(2,1)S(1)}, s32[]{:S(2)}) %slice-start) | async-done | bytes 1572888 | tf_op jit(solution)/shard_map/slice | solution.py:494
  1.4 0.2 copy.19
  1.6 1.7 %fetch.1 = (bf16[256,768]{1,0:T(8,128)(2,1)S(1)}, f32[24,768]{1,0:T(8,128)S(1)}, bf16[256,2,768]{2,1,0:T(2,128)(2,1)S(1)}, bf16[1,8,384]{2,1,0:T(8,128)(2,1)S(1)...) custom-call(bf16[80,768]{1,0:T(8,128)(2,1)} %bitcast.14, ...), custom_call_target="tpu_custom_call" | custom-call | tf_op jit(solution)/shard_map/fetch/pallas_call | solution.py:446
  3.3 0.1 copy.20
  3.4 0.0 copy-start.2
  3.4 0.0 copy-start.1
  3.5 0.0 copy-start
  3.5 0.2 pad_maximum_fusion.in_mine
  3.6 0.6 %collective-permute-start.5 = (bf16[2,768,768]{2,1,0:T(8,128)(2,1)S(1)}, bf16[2,768,768]{2,1,0:T(8,128)(2,1)S(1)}, u32[]{:S(2)}, u32[]{:S(2)}) collective-permute-start(bf16[2,768,768]{2,1,0:T(8,128)(2,1)S(1)} %pad_maximum_fusion.in_mine), channel_id=1, source_target_pairs={{0,1},{1,0},{2,3},{3,2},{4,5},{5,4},{6,7},{7,6},{8,9},{9,8},{10,11... | collective-permute-start | bytes 7077896 | tf_op jit(solution)/shard_map/ppermute | solution.py:195
  4.2 0.0 copy-done.2
  4.2 3.7 %collective-permute-start.1 = (bf16[1,8,384]{2,1,0:T(8,128)(2,1)S(1)}, bf16[1,8,384]{2,1,0:T(8,128)(2,1)S(1)}, u32[]{:S(2)}, u32[]{:S(2)}) collective-permute-start(bf16[1,8,384]{2,1,0:T(8,128)(2,1)S(1)} %copy-done.2), channel_id=1, source_target_pairs={{0,9},{1,8},{2,11},{3,10},{4,13},{5,12},{6,15},{7,14},{8,1},{9,0},... | collective-permute-start | bytes 18440 | tf_op jit(solution)/shard_map/ppermute | solution.py:491
  7.9 0.4 %collective-permute-start.6 = (f32[24,768]{1,0:T(8,128)S(1)}, f32[24,768]{1,0:T(8,128)S(1)}, u32[]{:S(2)}, u32[]{:S(2)}) collective-permute-start(f32[24,768]{1,0:T(8,128)S(1)} %get-tuple-element.17.wide_mine), channel_id=1, source_target_pairs={{0,1},{1,0},{2,3},{3,2},{4,5},{5,4},{6,7},{7,6},{8,9},{9,8},{10,11... | collective-permute-start | bytes 221192 | tf_op jit(solution)/shard_map/ppermute | solution.py:195
  8.3 0.1 collective-permute-start
  8.4 0.4 %collective-permute-start.7 = (bf16[768,384]{1,0:T(8,128)(2,1)S(1)}, bf16[768,384]{1,0:T(8,128)(2,1)S(1)}, u32[]{:S(2)}, u32[]{:S(2)}) collective-permute-start(bf16[768,384]{1,0:T(8,128)(2,1)S(1)} %get-tuple-element.18), channel_id=1, source_target_pairs={{0,1},{1,0},{2,3},{3,2},{4,5},{5,4},{6,7},{7,6},{8,9},{9,8},{10,11... | collective-permute-start | bytes 1769480 | tf_op jit(solution)/shard_map/ppermute | solution.py:195
  9.5 0.0 collective-permute-done.1
  9.5 1.3 %collective-permute-start.2 = (bf16[2,8,384]{2,1,0:T(8,128)(2,1)S(1)}, bf16[2,8,384]{2,1,0:T(8,128)(2,1)S(1)}, u32[]{:S(2)}, u32[]{:S(2)}) collective-permute-start(bf16[2,8,384]{2,1,0:T(8,128)(2,1)S(1)} %pad_maximum_fusion.2), channel_id=1, source_target_pairs={{0,3},{1,2},{2,1},{3,0},{4,7},{5,6},{6,5},{7,4},{8,11},{9,10},{10,... | collective-permute-start | bytes 36872 | tf_op jit(solution)/shard_map/ppermute | solution.py:491
  10.8 1.9 %collective-permute-done.2 = bf16[2,8,384]{2,1,0:T(8,128)(2,1)S(1)} collective-permute-done((bf16[2,8,384]{2,1,0:T(8,128)(2,1)S(1)}, bf16[2,8,384]{2,1,0:T(8,128)(2,1)S(1)}, u32[]{:S(2)}, u32[]{:S(2)}) %collective-permute-start.2) | collective-permute-done | bytes 12320 | tf_op jit(solution)/shard_map/ppermute | solution.py:491
  12.7 1.4 %collective-permute-start.3 = (bf16[4,8,384]{2,1,0:T(8,128)(2,1)S(1)}, bf16[4,8,384]{2,1,0:T(8,128)(2,1)S(1)}, u32[]{:S(2)}, u32[]{:S(2)}) collective-permute-start(bf16[4,8,384]{2,1,0:T(8,128)(2,1)S(1)} %pad_maximum_fusion.1), channel_id=1, source_target_pairs={{0,5},{1,4},{2,7},{3,6},{4,1},{5,0},{6,3},{7,2},{8,13},{9,12},{10,... | collective-permute-start | bytes 73736 | tf_op jit(solution)/shard_map/ppermute | solution.py:491
  14.1 1.9 %collective-permute-done.3 = bf16[4,8,384]{2,1,0:T(8,128)(2,1)S(1)} collective-permute-done((bf16[4,8,384]{2,1,0:T(8,128)(2,1)S(1)}, bf16[4,8,384]{2,1,0:T(8,128)(2,1)S(1)}, u32[]{:S(2)}, u32[]{:S(2)}) %collective-permute-start.3) | collective-permute-done | bytes 24608 | tf_op jit(solution)/shard_map/ppermute | solution.py:491
  16.0 0.1 collective-permute-start.4
  16.1 0.0 collective-permute-done.narrow_ref.narrow_other
  16.2 0.0 copy-done.1
  16.2 0.3 %prepare.1.rows_ref = f32[8,384]{1,0:T(8,128)S(1)} custom-call(f32[1,64]{1,0:T(1,128)S(1)} %exponential_multiply_fusion.angle_ref, bf16[3,128,384]{2,1,0:T(8,128)(2,1)S(1)} %bitcast.11, bf16[256,768]{1,0:T(8,128)(2,1)S(1)} %collective-permute-done.narrow_ref.narrow_other), custom_call_target="tpu_custom_call" | custom-call | tf_op jit(solution)/shard_map/prepare/pallas_call | solution.py:502
  16.5 0.0 collective-permute-done.6.wide_other
  16.5 0.8 %collective-permute-done.4.other_ref = bf16[8,8,384]{2,1,0:T(8,128)(2,1)S(1)} collective-permute-done((bf16[8,8,384]{2,1,0:T(8,128)(2,1)S(1)}, bf16[8,8,384]{2,1,0:T(8,128)(2,1)S(1)}, u32[]{:S(2)}, u32[]{:S(2)}) %collective-permute-start.4) | collective-permute-done | bytes 49184 | tf_op jit(solution)/shard_map/ppermute | solution.py:195
  17.3 0.0 collective-permute-done.7.out_other
  17.3 0.0 collective-permute-done.5.in_other
  17.3 0.0 copy-done
  17.3 3.0 %scan_block.1 = bf16[8,384]{1,0:T(8,128)(2,1)} custom-call(bf16[2,64,128]{2,1,0:T(8,128)(2,1)S(1)} %get-tuple-element.12.pick_ref, f32[64,128]{1,0:T(8,128)S(1)} %get-tuple-element.13.live_ref, f32[8,384]{1,0:T(8,128)S(1)} %prepare.1.rows_ref, bf16[8,8,384]{2,1,0:T(8,128)(2,1)S(1)} %constant_dynamic-update-slice_fusion.mine_ref, ...), custom_call_target="tpu_custom_call" | custom-call | tf_op jit(solution)/shard_map/scan_block/pallas_call | solution.py:525
  (7 shorter events, 0.1 us)
Async XLA Ops:
  0.0 1.4 %slice-start = ((bf16[768,2,768]{2,1,0:T(2,128)(2,1)}), bf16[512,2,768]{2,1,0:T(2,128)(2,1)S(1)}, s32[]{:S(2)}) async-start(bf16[768,2,768]{2,1,0:T(2,128)(2,1)} %into_ref.1), calls=%async_computation | async-start | bytes 3145728 | tf_op jit(solution)/shard_map/slice | solution.py:494
  3.4 0.8 %copy-start.2 = (bf16[1,8,384]{2,1,0:T(8,128)(2,1)S(1)}, bf16[1,8,384]{2,1,0:T(8,128)(2,1)}, u32[]{:S(2)}) copy-start(bf16[1,8,384]{2,1,0:T(8,128)(2,1)} %latent_ref.1) | copy-start | bytes 18436
  3.4 12.7 %copy-start.1 = (bf16[128,3,384]{2,0,1:T(8,128)(2,1)S(1)}, bf16[128,3,384]{2,0,1:T(8,128)(2,1)}, u32[]{:S(2)}) copy-start(bf16[128,3,384]{2,0,1:T(8,128)(2,1)} %param.16) | copy-start | bytes 884740
  3.5 13.8 %copy-start = (bf16[768,768]{1,0:T(8,128)(2,1)S(1)}, bf16[768,768]{1,0:T(8,128)(2,1)}, u32[]{:S(2)}) copy-start(bf16[768,768]{1,0:T(8,128)(2,1)} %out_mine.1) | copy-start | bytes 3538948
  3.6 13.6 %collective-permute-start.5 = (bf16[2,768,768]{2,1,0:T(8,128)(2,1)S(1)}, bf16[2,768,768]{2,1,0:T(8,128)(2,1)S(1)}, u32[]{:S(2)}, u32[]{:S(2)}) collective-permute-start(bf16[2,768,768]{2,1,0:T(8,128)(2,1)S(1)} %pad_maximum_fusion.in_mine), channel_id=1, source_target_pairs={{0,1},{1,0},{2,3},{3,2},{4,5},{5,4},{6,7},{7,6},{8,9},{9,8},{10,11... | collective-permute-start | bytes 7077896 | tf_op jit(solution)/shard_map/ppermute | solution.py:195
  4.2 5.3 %collective-permute-start.1 = (bf16[1,8,384]{2,1,0:T(8,128)(2,1)S(1)}, bf16[1,8,384]{2,1,0:T(8,128)(2,1)S(1)}, u32[]{:S(2)}, u32[]{:S(2)}) collective-permute-start(bf16[1,8,384]{2,1,0:T(8,128)(2,1)S(1)} %copy-done.2), channel_id=1, source_target_pairs={{0,9},{1,8},{2,11},{3,10},{4,13},{5,12},{6,15},{7,14},{8,1},{9,0},... | collective-permute-start | bytes 18440 | tf_op jit(solution)/shard_map/ppermute | solution.py:491
  7.9 8.6 %collective-permute-start.6 = (f32[24,768]{1,0:T(8,128)S(1)}, f32[24,768]{1,0:T(8,128)S(1)}, u32[]{:S(2)}, u32[]{:S(2)}) collective-permute-start(f32[24,768]{1,0:T(8,128)S(1)} %get-tuple-element.17.wide_mine), channel_id=1, source_target_pairs={{0,1},{1,0},{2,3},{3,2},{4,5},{5,4},{6,7},{7,6},{8,9},{9,8},{10,11... | collective-permute-start | bytes 221192 | tf_op jit(solution)/shard_map/ppermute | solution.py:195
  8.3 7.8 %collective-permute-start = (bf16[256,768]{1,0:T(8,128)(2,1)S(1)}, bf16[256,768]{1,0:T(8,128)(2,1)S(1)}, u32[]{:S(2)}, u32[]{:S(2)}) collective-permute-start(bf16[256,768]{1,0:T(8,128)(2,1)S(1)} %get-tuple-element.14.narrow_mine), channel_id=1, source_target_pairs={{0,1},{1,0},{2,3},{3,2},{4,5},{5,4},{6,7},{7,6},{8,9},{9,8},{10,11... | collective-permute-start | bytes 1179656 | tf_op jit(solution)/shard_map/ppermute | solution.py:195
  8.4 8.9 %collective-permute-start.7 = (bf16[768,384]{1,0:T(8,128)(2,1)S(1)}, bf16[768,384]{1,0:T(8,128)(2,1)S(1)}, u32[]{:S(2)}, u32[]{:S(2)}) collective-permute-start(bf16[768,384]{1,0:T(8,128)(2,1)S(1)} %get-tuple-element.18), channel_id=1, source_target_pairs={{0,1},{1,0},{2,3},{3,2},{4,5},{5,4},{6,7},{7,6},{8,9},{9,8},{10,11... | collective-permute-start | bytes 1769480 | tf_op jit(solution)/shard_map/ppermute | solution.py:195
  9.5 3.2 %collective-permute-start.2 = (bf16[2,8,384]{2,1,0:T(8,128)(2,1)S(1)}, bf16[2,8,384]{2,1,0:T(8,128)(2,1)S(1)}, u32[]{:S(2)}, u32[]{:S(2)}) collective-permute-start(bf16[2,8,384]{2,1,0:T(8,128)(2,1)S(1)} %pad_maximum_fusion.2), channel_id=1, source_target_pairs={{0,3},{1,2},{2,1},{3,0},{4,7},{5,6},{6,5},{7,4},{8,11},{9,10},{10,... | collective-permute-start | bytes 36872 | tf_op jit(solution)/shard_map/ppermute | solution.py:491
  12.7 3.3 %collective-permute-start.3 = (bf16[4,8,384]{2,1,0:T(8,128)(2,1)S(1)}, bf16[4,8,384]{2,1,0:T(8,128)(2,1)S(1)}, u32[]{:S(2)}, u32[]{:S(2)}) collective-permute-start(bf16[4,8,384]{2,1,0:T(8,128)(2,1)S(1)} %pad_maximum_fusion.1), channel_id=1, source_target_pairs={{0,5},{1,4},{2,7},{3,6},{4,1},{5,0},{6,3},{7,2},{8,13},{9,12},{10,... | collective-permute-start | bytes 73736 | tf_op jit(solution)/shard_map/ppermute | solution.py:491
  16.0 1.2 %collective-permute-start.4 = (bf16[8,8,384]{2,1,0:T(8,128)(2,1)S(1)}, bf16[8,8,384]{2,1,0:T(8,128)(2,1)S(1)}, u32[]{:S(2)}, u32[]{:S(2)}) collective-permute-start(bf16[8,8,384]{2,1,0:T(8,128)(2,1)S(1)} %constant_dynamic-update-slice_fusion.mine_ref), channel_id=1, source_target_pairs={{0,1},{1,0},{2,3},{3,2},{4,5},{5,4},{6,7},{7,6},{8,9},{9,8},{10,11... | collective-permute-start | bytes 147464 | tf_op jit(solution)/shard_map/ppermute | solution.py:195
